TPU v7x, 256 devices: a whole 4x4x8 slice. The times are simulated.
256 devices in a mesh: ctx: 128 (over y, z, x_lo, core), head: 2 (over x_hi).
Axes of the slice: x: 4 (x_hi: 2, x_lo: 2; x = x_hi * 2 + x_lo), y: 4, z: 8, core: 2. Of those that a mesh axis runs over, the one named last changes fastest.
Arguments:
- queries: bfloat16 [16384, 2048], P('ctx', 'head'), may hold values from -6 to 6
- key_states: bfloat16 [16384, 512], P(('ctx', 'head')), may hold values from -6 to 6
- value_states: bfloat16 [16384, 512], P(('ctx', 'head')), may hold values from -6 to 6
- attn_out: bfloat16 [16384, 2048], P('ctx', 'head'), may hold values from -1.5 to 1.5
- grad_out: bfloat16 [16384, 2048], P('ctx', 'head'), may hold values from -24 to 24
- log_sum_exp: float32 [16, 16384], P('head', 'ctx')
- token_order: int32 [16384], P('ctx'), may hold values from 0 to 16383, as said below
- position: int32 [16384], P('ctx'), may hold values from 0 to 4095, as said below
Outputs:
- grad_queries: bfloat16 [16384, 2048], P('ctx', 'head')
- grad_keys: bfloat16 [16384, 512], P(('ctx', 'head'))
- grad_values: bfloat16 [16384, 512], P(('ctx', 'head'))
Inputs may be any that keep to these rules, and one draw needn't show every extreme that they name: `token_order`: a permutation of the sequence positions; the 128 rows of ctx index d hold consecutive positions in increasing order, all within quarter d mod 4 of the sequence (quarter k holds positions k * 4096 to (k + 1) * 4096 - 1). Documents are runs of consecutive sequence positions that never cross a multiple of 4096; token_order[r] - position[r] is the sequence position where row r's document starts; some document fills a whole quarter.
All inputs are finite; a program needn't handle non-finite values.
Results may differ from a plain program's by a relative error of at most 0.0055.
Values may be sent and summed in bfloat16 or wider, within the bound.
No kernel may reach another device: no remote copies, remote signals or barrier semaphores. Data moves between devices by JAX's collectives and lax.ppermute only.
A program may use at most 64 MiB of HBM per device.

v0:
```python
import functools
import math

import jax
import jax.numpy as jnp
from jax import lax
from jax.experimental import pallas as pl
from jax.experimental.pallas import tpu as pltpu
from jax.sharding import PartitionSpec as P


HEAD_DIM = 128
QUARTERS = 4
GRID_Y = 4
GRID_Z = 8
ROW_SHIFTS = (0, 1, -1, 2)
AUX = 16
LOG2E = math.log2(math.e)
SCALE = HEAD_DIM ** (-0.5)

VMEM_SPEC = pl.BlockSpec(memory_space=pltpu.VMEM)
SMEM_SPEC = pl.BlockSpec(memory_space=pltpu.SMEM)
NT = (((1,), (1,)), ((), ()))
NN = (((1,), (0,)), ((), ()))


def dot(a, b, dims):
    return lax.dot_general(a, b, dims, preferred_element_type=jnp.float32)


def shifted(value, along_y, along_z):
    pairs = []
    for y in range(GRID_Y):
        for z in range(GRID_Z):
            source = ((y + along_y) % GRID_Y) * GRID_Z + (z + along_z) % GRID_Z
            for quarter in range(QUARTERS):
                pairs.append((source * QUARTERS + quarter, (y * GRID_Z + z) * QUARTERS + quarter))
    return lax.ppermute(value, "ctx", pairs)


def swap_head(value):
    return lax.ppermute(value, "head", [(0, 1), (1, 0)])


def split_three(x):
    high = x.astype(jnp.bfloat16)
    rest = x - high.astype(jnp.float32)
    middle = rest.astype(jnp.bfloat16)
    low = (rest - middle.astype(jnp.float32)).astype(jnp.bfloat16)
    return high, middle, low


def split_place(x):
    return (x >> 7).astype(jnp.float32).astype(jnp.bfloat16), (x & 127).astype(jnp.float32).astype(jnp.bfloat16)


def pack_rows_kernel(q_ref, o_ref, g_ref, lse_ref, order_ref, position_ref, out_ref):
    rows, width = q_ref.shape
    out_ref[0:rows, :] = q_ref[...]
    out_ref[rows : 2 * rows, :] = g_ref[...]
    base = 2 * rows
    out_ref[base : base + AUX, :] = jnp.zeros((AUX, width), jnp.bfloat16)
    order = order_ref[...]
    first = order - position_ref[...]
    places = split_place(first) + split_place(order)
    for at, part in enumerate(places):
        out_ref[base + 6 : base + 7, at * rows : (at + 1) * rows] = part
    product = q_ref.shape[1] // HEAD_DIM
    for h in range(product):
        span = slice(h * HEAD_DIM, (h + 1) * HEAD_DIM)
        both = g_ref[:, span].astype(jnp.float32) * o_ref[:, span].astype(jnp.float32)
        out_dot = jnp.sum(jnp.transpose(both), axis=0, keepdims=True)
        for at, part in enumerate(split_three(lse_ref[h : h + 1, :])):
            out_ref[base + at : base + at + 1, span] = part
        for at, part in enumerate(split_three(out_dot)):
            out_ref[base + 3 + at : base + 4 + at, span] = part


def pick_kernel(head_ref, k_ref, v_ref, keep_ref, send_ref):
    width = k_ref.shape[1] // 2
    head = head_ref[0]

    def fill(mine, other):
        keep_ref[:, :width] = k_ref[:, mine * width : (mine + 1) * width]
        keep_ref[:, width:] = v_ref[:, mine * width : (mine + 1) * width]
        send_ref[:, :width] = k_ref[:, other * width : (other + 1) * width]
        send_ref[:, width:] = v_ref[:, other * width : (other + 1) * width]

    pl.when(head == 0)(lambda: fill(0, 1))
    pl.when(head != 0)(lambda: fill(1, 0))


def pack_cols_kernel(head_ref, keep_ref, got_ref, order_ref, out_ref):
    half, width = keep_ref.shape
    head = head_ref[0]

    @pl.when(head == 0)
    def _():
        out_ref[0:half, :] = keep_ref[...]
        out_ref[half : 2 * half, :] = got_ref[...]

    @pl.when(head != 0)
    def _():
        out_ref[0:half, :] = got_ref[...]
        out_ref[half : 2 * half, :] = keep_ref[...]

    base = 2 * half
    out_ref[base : base + AUX, :] = jnp.zeros((AUX, width), jnp.bfloat16)
    for at, part in enumerate(split_place(order_ref[...])):
        out_ref[base : base + 1, at * 2 * half : (at + 1) * 2 * half] = part


def grads_kernel(n_rows, col_places, done_rows, done_cols, given, final, *refs):
    n_cols = len(col_places)
    n_col_refs = 1 + max(at for at, _ in col_places)
    refs = list(refs)

    def take(count):
        taken, refs[:] = refs[:count], refs[count:]
        return taken

    row_refs = take(n_rows)
    col_refs = take(n_col_refs)
    sums_in = take(3) if given else None
    if final:
        dq_refs = take(n_rows)
        dkv_refs = take(n_cols)
    else:
        sums_out = take(3)
    qs, gs, lse_s, dot_s, first_s, last_s, ks, vs, kts = take(9)
    if final:
        dqt, dk, dv = take(3)
    else:
        dqt, dk, dv = sums_out
    starts, listed, counts = take(3)
    rows = 128
    heads = row_refs[0].shape[1] // HEAD_DIM
    kv_heads = col_refs[0].shape[1] // HEAD_DIM // 2
    group = heads // kv_heads
    wide = group * rows

    eye_i = lax.broadcasted_iota(jnp.int32, (rows, rows), 0)
    eye_j = lax.broadcasted_iota(jnp.int32, (rows, rows), 1)
    eye = (eye_i == eye_j).astype(jnp.float32).astype(jnp.bfloat16)

    col_starts = []
    for c, (at, base) in enumerate(col_places):
        ref = col_refs[at]
        for j in range(kv_heads):
            k = ref[base : base + rows, j * HEAD_DIM : (j + 1) * HEAD_DIM]
            ks[c, j] = k
            vs[c, j] = ref[base : base + rows, (kv_heads + j) * HEAD_DIM : (kv_heads + j + 1) * HEAD_DIM]
            kts[c, j] = dot(eye, k, NT).astype(jnp.bfloat16)
        aux = ref[base + rows : base + rows + AUX, :].astype(jnp.float32)
        place = (aux[0:1, 0:rows] * 128.0 + aux[0:1, rows : 2 * rows]).astype(jnp.int32)
        col_starts.append(jnp.min(place))
        starts[c] = col_starts[-1]
    for r, ref in enumerate(row_refs):
        base = 2 * rows
        for h in range(heads):
            span = slice(h * HEAD_DIM, (h + 1) * HEAD_DIM)
            qs[r, span, :] = ref[0:rows, span]
            gs[r, span, :] = ref[rows : 2 * rows, span]
        aux = ref[base : base + AUX, :].astype(jnp.float32)
        lse = (aux[0:1] + aux[1:2]) + aux[2:3]
        out_dot = (aux[3:4] + aux[4:5]) + aux[5:6]
        lse_s[r] = lse * LOG2E
        dot_s[r] = out_dot
        first = aux[6:7, 0:rows] * 128.0 + aux[6:7, rows : 2 * rows]
        last = aux[6:7, 2 * rows : 3 * rows] * 128.0 + aux[6:7, 3 * rows : 4 * rows]
        first = first.astype(jnp.int32)
        last = last.astype(jnp.int32)
        for g in range(group):
            first_s[r, :, g * rows : (g + 1) * rows] = first
            last_s[r, :, g * rows : (g + 1) * rows] = last
        most = jnp.max(last)
        least = jnp.min(first)
        count = jnp.int32(0)
        for c in range(n_cols):
            if r < done_rows and c < done_cols:
                continue
            listed[r, count] = c
            some = (col_starts[c] <= most) & (col_starts[c] + (rows - 1) >= least)
            count = count + some.astype(jnp.int32)
        counts[r] = count
    if given:
        for old, new in zip(sums_in, (dqt, dk, dv)):
            have = old.shape[0]
            new[0:have] = old[...]
            new[have:] = jnp.zeros((new.shape[0] - have,) + new.shape[1:], jnp.float32)
    else:
        dqt[...] = jnp.zeros_like(dqt)
        dk[...] = jnp.zeros_like(dk)
        dv[...] = jnp.zeros_like(dv)

    def pair(r, one, two, start_one, start_two):
        along = lax.broadcasted_iota(jnp.int32, (rows, wide), 0)
        last = last_s[r]
        first = first_s[r]
        visible = [
            (along + start <= last) & (along + start >= first) for start in (start_one, start_two)
        ]
        for j in range(kv_heads):
            span = slice(j * wide, (j + 1) * wide)
            q = qs[r, span, :]
            g = gs[r, span, :]
            keys = jnp.concatenate([ks[one, j], ks[two, j]], axis=0)
            values = jnp.concatenate([vs[one, j], vs[two, j]], axis=0)
            keys_turned = jnp.concatenate([kts[one, j], kts[two, j]], axis=1)
            scores = dot(keys, q, NT)
            prob_grad = dot(values, g, NT)
            lse = lse_s[r, :, span]
            out_dot = dot_s[r, :, span]
            probs_both = []
            grads_both = []
            for at in range(2):
                part = slice(at * rows, (at + 1) * rows)
                probs = jnp.exp2(scores[part] * (SCALE * LOG2E) - lse)
                probs = jnp.where(visible[at], probs, 0.0)
                grads_both.append((probs * (prob_grad[part] - out_dot) * SCALE).astype(jnp.bfloat16))
                probs_both.append(probs.astype(jnp.bfloat16))
            probs = jnp.concatenate(probs_both, axis=0)
            score_grad = jnp.concatenate(grads_both, axis=0)
            value_update = dot(probs, g, NN)
            key_update = dot(score_grad, q, NN)
            dv[one, j] += value_update[:rows]
            dv[two, j] += value_update[rows:]
            dk[one, j] += key_update[:rows]
            dk[two, j] += key_update[rows:]
            dqt[r, j] += dot(keys_turned, score_grad, NN)

    def row_block(r, carry):
        count = counts[r]

        def trip(at, inner):
            one = listed[r, 2 * at]
            both = 2 * at + 1 < count
            two = jnp.where(both, listed[r, 2 * at + 1], one)
            pair(r, one, two, starts[one], jnp.where(both, starts[two], 1 << 20))
            return inner

        return lax.fori_loop(0, (count + 1) // 2, trip, carry)

    lax.fori_loop(0, n_rows, row_block, 0)

    if not final:
        return
    for c, ref in enumerate(dkv_refs):
        for j in range(kv_heads):
            ref[:, j * HEAD_DIM : (j + 1) * HEAD_DIM] = dk[c, j].astype(jnp.bfloat16)
            ref[:, (kv_heads + j) * HEAD_DIM : (kv_heads + j + 1) * HEAD_DIM] = dv[c, j].astype(jnp.bfloat16)
    for r, ref in enumerate(dq_refs):
        for j in range(kv_heads):
            for g in range(group):
                part = dqt[r, j, :, g * rows : (g + 1) * rows].astype(jnp.bfloat16)
                h = j * group + g
                ref[:, h * HEAD_DIM : (h + 1) * HEAD_DIM] = dot(eye, part, NT).astype(jnp.bfloat16)


def call_grads(row_packs, col_packs, col_places, done, sums, final, rows, width, kv_width):
    n_rows, n_cols = len(row_packs), len(col_places)
    kv_heads = kv_width // HEAD_DIM
    heads = width // HEAD_DIM
    wide = heads // kv_heads * rows
    shape = jax.ShapeDtypeStruct
    sum_shapes = (
        (n_rows, kv_heads, HEAD_DIM, wide),
        (n_cols, kv_heads, rows, HEAD_DIM),
        (n_cols, kv_heads, rows, HEAD_DIM),
    )
    if final:
        out_shape = (shape((rows, width), jnp.bfloat16),) * n_rows
        out_shape += (shape((rows, 2 * kv_width), jnp.bfloat16),) * n_cols
    else:
        out_shape = tuple(shape(s, jnp.float32) for s in sum_shapes)
    operands = (*row_packs, *col_packs, *sums)
    scratch = [
        pltpu.VMEM((n_rows, heads * rows, HEAD_DIM), jnp.bfloat16),
        pltpu.VMEM((n_rows, heads * rows, HEAD_DIM), jnp.bfloat16),
        pltpu.VMEM((n_rows, 1, heads * rows), jnp.float32),
        pltpu.VMEM((n_rows, 1, heads * rows), jnp.float32),
        pltpu.VMEM((n_rows, 1, wide), jnp.int32),
        pltpu.VMEM((n_rows, 1, wide), jnp.int32),
        pltpu.VMEM((n_cols, kv_heads, rows, HEAD_DIM), jnp.bfloat16),
        pltpu.VMEM((n_cols, kv_heads, rows, HEAD_DIM), jnp.bfloat16),
        pltpu.VMEM((n_cols, kv_heads, HEAD_DIM, rows), jnp.bfloat16),
    ]
    if final:
        scratch += [pltpu.VMEM(s, jnp.float32) for s in sum_shapes]
    scratch += [
        pltpu.SMEM((n_cols,), jnp.int32),
        pltpu.SMEM((n_rows, n_cols + 1), jnp.int32),
        pltpu.SMEM((n_rows,), jnp.int32),
    ]
    body = functools.partial(grads_kernel, n_rows, col_places, *done, bool(sums), final)
    return pl.pallas_call(
        body,
        out_shape=out_shape,
        in_specs=[VMEM_SPEC] * len(operands),
        out_specs=(VMEM_SPEC,) * len(out_shape),
        scratch_shapes=scratch,
        compiler_params=pltpu.CompilerParams(vmem_limit_bytes=40 * 1024 * 1024),
    )(*operands)


def shards(queries, key_states, value_states, attn_out, grad_out, log_sum_exp, token_order, position):
    rows, width = queries.shape
    half, all_width = key_states.shape
    kv_width = all_width // 2
    head = lax.axis_index("head").astype(jnp.int32)[None]
    order = token_order[None]
    shape = jax.ShapeDtypeStruct

    keep, send = pl.pallas_call(
        pick_kernel,
        out_shape=(shape((half, 2 * kv_width), jnp.bfloat16),) * 2,
        in_specs=[SMEM_SPEC, VMEM_SPEC, VMEM_SPEC],
        out_specs=(VMEM_SPEC,) * 2,
    )(head, key_states, value_states)
    got = swap_head(send)
    row_pack = pl.pallas_call(
        pack_rows_kernel,
        out_shape=shape((2 * rows + AUX, width), jnp.bfloat16),
        in_specs=[VMEM_SPEC] * 6,
        out_specs=VMEM_SPEC,
    )(queries, attn_out, grad_out, log_sum_exp, order, position[None])
    col_pack = pl.pallas_call(
        pack_cols_kernel,
        out_shape=shape((2 * half + AUX, 2 * kv_width), jnp.bfloat16),
        in_specs=[SMEM_SPEC, VMEM_SPEC, VMEM_SPEC, VMEM_SPEC],
        out_specs=VMEM_SPEC,
    )(head, keep, got, order)

    row_packs = [row_pack]
    for s in (1, -1, 2):
        row_packs.append(shifted(row_pack, s, 0))
    ahead = shifted(col_pack, 0, 1)
    behind = shifted(col_pack, 0, -1)
    across = shifted(col_pack, 0, 4)
    ahead_pair = shifted(jnp.concatenate([col_pack, ahead], axis=0), 0, 2)
    behind_pair = shifted(jnp.concatenate([col_pack, behind], axis=0), 0, -2)
    size = 2 * half + AUX
    near_places = ((0, 0), (1, 0), (2, 0), (3, 0))
    far_places = ((4, 0), (4, size), (5, 0), (5, size))
    col_shifts = (0, 1, -1, 4, 2, 3, -2, -3)
    near = [col_pack, ahead, behind, across]

    sums = call_grads(row_packs[:3], near, near_places, (0, 0), (), False, rows, width, kv_width)
    outs = call_grads(
        row_packs,
        near + [ahead_pair, behind_pair],
        near_places + far_places,
        (3, 4),
        sums,
        True,
        rows,
        width,
        kv_width,
    )
    n_rows = len(ROW_SHIFTS)
    dq_parts, dkv_parts = outs[:n_rows], outs[n_rows:]

    dkv = dkv_parts[0].astype(jnp.float32)
    for s, part in list(zip(col_shifts, dkv_parts))[1:]:
        back = shifted(part, 0, -s)
        dkv = dkv + back.astype(jnp.float32)
    dq = dq_parts[0].astype(jnp.float32)
    for s, part in list(zip(ROW_SHIFTS, dq_parts))[1:]:
        back = shifted(part, -s, 0)
        dq = dq + back.astype(jnp.float32)
    grad_queries = dq.astype(jnp.bfloat16)

    dkv = dkv.astype(jnp.bfloat16)
    is_first = head[0] == 0
    send_back = jnp.where(is_first, dkv[half:], dkv[:half])
    mine = jnp.where(is_first, dkv[:half], dkv[half:])
    other = swap_head(send_back)
    low = jnp.where(is_first, mine, other)
    high = jnp.where(is_first, other, mine)
    grad_keys = jnp.concatenate([low[:, :kv_width], high[:, :kv_width]], axis=1)
    grad_values = jnp.concatenate([low[:, kv_width:], high[:, kv_width:]], axis=1)
    return grad_queries, grad_keys, grad_values


def solution(mesh):
    in_specs = (
        P("ctx", "head"),
        P(("ctx", "head"), None),
        P(("ctx", "head"), None),
        P("ctx", "head"),
        P("ctx", "head"),
        P("head", "ctx"),
        P("ctx"),
        P("ctx"),
    )
    out_specs = (P("ctx", "head"), P(("ctx", "head"), None), P(("ctx", "head"), None))
    return jax.shard_map(shards, mesh=mesh, in_specs=in_specs, out_specs=out_specs, check_vma=False)
```

profile of v0, /device:TPU:2, one launch (start us, length us, event | category | flops | bytes accessed | tf_op | source)
XLA Modules:
  0.0 97.7 jit_solution(2708605179015110857)
XLA Ops:
  0.6 1.5 %shard_map.104 = (bf16[64,512]{1,0:T(8,128)(2,1)}, bf16[64,512]{1,0:T(8,128)(2,1)}) custom-call(s32[1]{0:T(128)} %bitcast.2.head_ref, bf16[64,512]{1,0:T(8,128)(2,1)} %k_ref.1, bf16[64,512]{1,0:T(8,128)(2,1)} %v_ref.1), custom_call_target="tpu_custom_call" | custom-call | tf_op jit(solution)/shard_map/pallas_call | solution.py:314
  2.2 2.1 %collective-permute-start.3 = (bf16[64,512]{1,0:T(8,128)(2,1)}, bf16[64,512]{1,0:T(8,128)(2,1)S(1)}, u32[]{:S(2)}, u32[]{:S(2)}) collective-permute-start(bf16[64,512]{1,0:T(8,128)(2,1)} %get-tuple-element.21), channel_id=1, source_target_pairs={{0,1},{1,0},{2,3},{3,2},{4,5},{5,4},{6,7},{7,6},{8,9},{9,8},{10,11... | collective-permute-start | bytes 196616 | tf_op jit(solution)/shard_map/ppermute | solution.py:42
  4.3 3.9 %collective-permute-done.3.got_ref = bf16[64,512]{1,0:T(8,128)(2,1)S(1)} collective-permute-done((bf16[64,512]{1,0:T(8,128)(2,1)}, bf16[64,512]{1,0:T(8,128)(2,1)S(1)}, u32[]{:S(2)}, u32[]{:S(2)}) %collective-permute-start.3) | collective-permute-done | bytes 65568 | tf_op jit(solution)/shard_map/ppermute | solution.py:42
  8.8 1.6 %shard_map.105.refs_3_.refs_4_ = bf16[144,512]{1,0:T(8,128)(2,1)} custom-call(s32[1]{0:T(128)} %bitcast.2.head_ref, bf16[64,512]{1,0:T(8,128)(2,1)} %get-tuple-element.20.keep_ref, bf16[64,512]{1,0:T(8,128)(2,1)} %copy-done.3, s32[1,128]{1,0:T(1,128)} %bitcast.3), custom_call_target="tpu_custom_call" | custom-call | tf_op jit(solution)/shard_map/pallas_call | solution.py:327
  10.3 1.9 %collective-permute-start.5 = (bf16[144,512]{1,0:T(8,128)(2,1)}, bf16[144,512]{1,0:T(8,128)(2,1)S(1)}, u32[]{:S(2)}, u32[]{:S(2)}) collective-permute-start(bf16[144,512]{1,0:T(8,128)(2,1)} %shard_map.105.refs_3_.refs_4_), channel_id=1, source_target_pairs={{56,0},{58,2},{60,4},{62,6},{0,8},{2,10},{4,12},{6,14},{8,16},{10,... | collective-permute-start | bytes 442376 | tf_op jit(solution)/shard_map/ppermute | solution.py:38
  12.2 3.9 %collective-permute-start.4 = (bf16[144,512]{1,0:T(8,128)(2,1)}, bf16[144,512]{1,0:T(8,128)(2,1)S(1)}, u32[]{:S(2)}, u32[]{:S(2)}) collective-permute-start(bf16[144,512]{1,0:T(8,128)(2,1)} %shard_map.105.refs_3_.refs_4_), channel_id=1, source_target_pairs={{8,0},{10,2},{12,4},{14,6},{16,8},{18,10},{20,12},{22,14},{24,16},... | collective-permute-start | bytes 442376 | tf_op jit(solution)/shard_map/ppermute | solution.py:38
  16.2 2.2 %shard_map.103.refs_0_ = bf16[272,1024]{1,0:T(8,128)(2,1)} custom-call(bf16[128,1024]{1,0:T(8,128)(2,1)} %q_ref.1, bf16[128,1024]{1,0:T(8,128)(2,1)} %o_ref.1, bf16[128,1024]{1,0:T(8,128)(2,1)} %g_ref.1, f32[8,128]{1,0:T(8,128)} %lse_ref.1, s32[1,128]{1,0:T(1,128)} %bitcast.4, s32[1,128]{1,0:T(1,128)} %bitcast.5), custom_call_target="tpu_custom_call" | custom-call | tf_op jit(solution)/shard_map/pallas_call | solution.py:321
  18.4 1.6 %collective-permute-start.1 = (bf16[272,1024]{1,0:T(8,128)(2,1)}, bf16[272,1024]{1,0:T(8,128)(2,1)S(1)}, u32[]{:S(2)}, u32[]{:S(2)}) collective-permute-start(bf16[272,1024]{1,0:T(8,128)(2,1)} %shard_map.103.refs_0_), channel_id=1, source_target_pairs={{192,0},{194,2},{196,4},{198,6},{200,8},{202,10},{204,12},{206,14}... | collective-permute-start | bytes 1671176 | tf_op jit(solution)/shard_map/ppermute | solution.py:38
  20.0 1.7 %collective-permute-start = (bf16[272,1024]{1,0:T(8,128)(2,1)}, bf16[272,1024]{1,0:T(8,128)(2,1)S(1)}, u32[]{:S(2)}, u32[]{:S(2)}) collective-permute-start(bf16[272,1024]{1,0:T(8,128)(2,1)} %shard_map.103.refs_0_), channel_id=1, source_target_pairs={{64,0},{66,2},{68,4},{70,6},{72,8},{74,10},{76,12},{78,14},{80,16}... | collective-permute-start | bytes 1671176 | tf_op jit(solution)/shard_map/ppermute | solution.py:38
  21.6 2.0 %collective-permute-start.2 = (bf16[272,1024]{1,0:T(8,128)(2,1)}, bf16[272,1024]{1,0:T(8,128)(2,1)S(1)}, u32[]{:S(2)}, u32[]{:S(2)}) collective-permute-start(bf16[272,1024]{1,0:T(8,128)(2,1)} %shard_map.103.refs_0_), channel_id=1, source_target_pairs={{128,0},{130,2},{132,4},{134,6},{136,8},{138,10},{140,12},{142,14}... | collective-permute-start | bytes 1671176 | tf_op jit(solution)/shard_map/ppermute | solution.py:38
  23.6 4.6 %collective-permute-start.6 = (bf16[144,512]{1,0:T(8,128)(2,1)}, bf16[144,512]{1,0:T(8,128)(2,1)S(1)}, u32[]{:S(2)}, u32[]{:S(2)}) collective-permute-start(bf16[144,512]{1,0:T(8,128)(2,1)} %shard_map.105.refs_3_.refs_4_), channel_id=1, source_target_pairs={{32,0},{34,2},{36,4},{38,6},{40,8},{42,10},{44,12},{46,14},{48,16}... | collective-permute-start | bytes 442376 | tf_op jit(solution)/shard_map/ppermute | solution.py:38
  28.2 1.0 %pad_maximum_fusion = (bf16[288,512]{1,0:T(8,128)(2,1)S(1)}, bf16[288,512]{1,0:T(8,128)(2,1)S(1)}) fusion(bf16[144,512]{1,0:T(8,128)(2,1)} %shard_map.105.refs_3_.refs_4_, bf16[144,512]{1,0:T(8,128)(2,1)S(1)} %collective-permute-done.5.refs_5_.refs_6_, bf16[144,512]{1,0:T(8,128)(2,1)S(1)} %collective-permute-done.4.refs_4_.refs_5_), kind=kLoop, calls=%fused_computation.1 | loop fusion | flops 1032192 | bytes 1032192 | tf_op jit(solution)/shard_map/concatenate | solution.py:341
  29.5 7.3 %collective-permute-done.6.refs_6_.refs_7_ = bf16[144,512]{1,0:T(8,128)(2,1)S(1)} collective-permute-done((bf16[144,512]{1,0:T(8,128)(2,1)}, bf16[144,512]{1,0:T(8,128)(2,1)S(1)}, u32[]{:S(2)}, u32[]{:S(2)}) %collective-permute-start.6) | collective-permute-done | bytes 147488 | tf_op jit(solution)/shard_map/ppermute | solution.py:38
  36.8 1.5 %collective-permute-start.7 = (bf16[288,512]{1,0:T(8,128)(2,1)S(1)}, bf16[288,512]{1,0:T(8,128)(2,1)S(1)}, u32[]{:S(2)}, u32[]{:S(2)}) collective-permute-start(bf16[288,512]{1,0:T(8,128)(2,1)S(1)} %get-tuple-element.40), channel_id=1, source_target_pairs={{16,0},{18,2},{20,4},{22,6},{24,8},{26,10},{28,12},{30,14},{32,16}... | collective-permute-start | bytes 884744 | tf_op jit(solution)/shard_map/ppermute | solution.py:38
  38.3 1.0 %copy-done = bf16[272,1024]{1,0:T(8,128)(2,1)S(1)} copy-done((bf16[272,1024]{1,0:T(8,128)(2,1)S(1)}, bf16[272,1024]{1,0:T(8,128)(2,1)}, u32[]{:S(2)}) %copy-start) | copy-done | bytes 557080
  39.4 3.5 %shard_map.106 = (f32[3,2,128,512]{3,2,1,0:T(8,128)S(1)}, f32[4,2,128,128]{3,2,1,0:T(8,128)S(1)}, f32[4,2,128,128]{3,2,1,0:T(8,128)S(1)}) custom-call(bf16[272,1024]{1,0:T(8,128)(2,1)S(1)} %copy-done, bf16[272,1024]{1,0:T(8,128)(2,1)S(1)} %collective-permute-done.refs_1_, bf16[272,1024]{1,0:T(8,128)(2,1)S(1)} %collective-permute-done.1.refs_2_, ...), custom_call_target="tpu_custom_call" | custom-call | tf_op jit(solution)/shard_map/pallas_call | solution.py:296
  42.9 3.5 %collective-permute-done.7.refs_8_ = bf16[288,512]{1,0:T(8,128)(2,1)S(1)} collective-permute-done((bf16[288,512]{1,0:T(8,128)(2,1)S(1)}, bf16[288,512]{1,0:T(8,128)(2,1)S(1)}, u32[]{:S(2)}, u32[]{:S(2)}) %collective-permute-start.7) | collective-permute-done | bytes 294944 | tf_op jit(solution)/shard_map/ppermute | solution.py:38
  46.4 3.0 %shard_map.107 = (bf16[128,1024]{1,0:T(8,128)(2,1)S(1)}, bf16[128,1024]{1,0:T(8,128)(2,1)S(1)}, bf16[128,1024]{1,0:T(8,128)(2,1)S(1)}, bf16[128,1024]{1,0:T(8,12...) custom-call(bf16[272,1024]{1,0:T(8,128)(2,1)S(1)} %copy-done.1, ...), custom_call_target="tpu_custom_call" | custom-call | tf_op jit(solution)/shard_map/pallas_call | solution.py:296
  49.4 3.9 %collective-permute-start.12 = (bf16[128,512]{1,0:T(8,128)(2,1)S(1)}, bf16[128,512]{1,0:T(8,128)(2,1)S(1)}, u32[]{:S(2)}, u32[]{:S(2)}) collective-permute-start(bf16[128,512]{1,0:T(8,128)(2,1)S(1)} %get-tuple-element.30), channel_id=1, source_target_pairs={{56,0},{58,2},{60,4},{62,6},{0,8},{2,10},{4,12},{6,14},{8,16},{10,... | collective-permute-start | bytes 393224 | tf_op jit(solution)/shard_map/ppermute | solution.py:38
  53.3 3.4 %collective-permute-start.13 = (bf16[128,512]{1,0:T(8,128)(2,1)S(1)}, bf16[128,512]{1,0:T(8,128)(2,1)S(1)}, u32[]{:S(2)}, u32[]{:S(2)}) collective-permute-start(bf16[128,512]{1,0:T(8,128)(2,1)S(1)} %get-tuple-element.31), channel_id=1, source_target_pairs={{8,0},{10,2},{12,4},{14,6},{16,8},{18,10},{20,12},{22,14},{24,16},... | collective-permute-start | bytes 393224 | tf_op jit(solution)/shard_map/ppermute | solution.py:38
  57.5 2.8 %collective-permute-start.15 = (bf16[128,512]{1,0:T(8,128)(2,1)S(1)}, bf16[128,512]{1,0:T(8,128)(2,1)S(1)}, u32[]{:S(2)}, u32[]{:S(2)}) collective-permute-start(bf16[128,512]{1,0:T(8,128)(2,1)S(1)} %get-tuple-element.33), channel_id=1, source_target_pairs={{48,0},{50,2},{52,4},{54,6},{56,8},{58,10},{60,12},{62,14},{0,16},... | collective-permute-start | bytes 393224 | tf_op jit(solution)/shard_map/ppermute | solution.py:38
  60.3 1.5 %collective-permute-start.16 = (bf16[128,512]{1,0:T(8,128)(2,1)S(1)}, bf16[128,512]{1,0:T(8,128)(2,1)S(1)}, u32[]{:S(2)}, u32[]{:S(2)}) collective-permute-start(bf16[128,512]{1,0:T(8,128)(2,1)S(1)} %get-tuple-element.34), channel_id=1, source_target_pairs={{40,0},{42,2},{44,4},{46,6},{48,8},{50,10},{52,12},{54,14},{56,16}... | collective-permute-start | bytes 393224 | tf_op jit(solution)/shard_map/ppermute | solution.py:38
  61.7 4.1 %collective-permute-start.17 = (bf16[128,512]{1,0:T(8,128)(2,1)S(1)}, bf16[128,512]{1,0:T(8,128)(2,1)S(1)}, u32[]{:S(2)}, u32[]{:S(2)}) collective-permute-start(bf16[128,512]{1,0:T(8,128)(2,1)S(1)} %get-tuple-element.35), channel_id=1, source_target_pairs={{16,0},{18,2},{20,4},{22,6},{24,8},{26,10},{28,12},{30,14},{32,16}... | collective-permute-start | bytes 393224 | tf_op jit(solution)/shard_map/ppermute | solution.py:38
  66.6 3.5 %collective-permute-done.14 = bf16[128,512]{1,0:T(8,128)(2,1)S(1)} collective-permute-done((bf16[128,512]{1,0:T(8,128)(2,1)S(1)}, bf16[128,512]{1,0:T(8,128)(2,1)S(1)}, u32[]{:S(2)}, u32[]{:S(2)}) %collective-permute-start.14) | collective-permute-done | bytes 131104 | tf_op jit(solution)/shard_map/ppermute | solution.py:38
  70.1 8.5 %collective-permute-done.15 = bf16[128,512]{1,0:T(8,128)(2,1)S(1)} collective-permute-done((bf16[128,512]{1,0:T(8,128)(2,1)S(1)}, bf16[128,512]{1,0:T(8,128)(2,1)S(1)}, u32[]{:S(2)}, u32[]{:S(2)}) %collective-permute-start.15) | collective-permute-done | bytes 131104 | tf_op jit(solution)/shard_map/ppermute | solution.py:38
  78.7 2.2 %collective-permute-done.18 = bf16[128,512]{1,0:T(8,128)(2,1)S(1)} collective-permute-done((bf16[128,512]{1,0:T(8,128)(2,1)S(1)}, bf16[128,512]{1,0:T(8,128)(2,1)S(1)}, u32[]{:S(2)}, u32[]{:S(2)}) %collective-permute-start.18) | collective-permute-done | bytes 131104 | tf_op jit(solution)/shard_map/ppermute | solution.py:38
  81.0 2.2 %collective-permute-start.19 = (bf16[64,512]{1,0:T(8,128)(2,1)S(1)}, bf16[64,512]{1,0:T(8,128)(2,1)S(1)}, u32[]{:S(2)}, u32[]{:S(2)}) collective-permute-start(bf16[64,512]{1,0:T(8,128)(2,1)S(1)} %broadcast_select_fusion.2), channel_id=1, source_target_pairs={{0,1},{1,0},{2,3},{3,2},{4,5},{5,4},{6,7},{7,6},{8,9},{9,8},{10,11... | collective-permute-start | bytes 196616 | tf_op jit(solution)/shard_map/ppermute | solution.py:42
  83.3 3.2 %collective-permute-start.10 = (bf16[128,1024]{1,0:T(8,128)(2,1)S(1)}, bf16[128,1024]{1,0:T(8,128)(2,1)S(1)}, u32[]{:S(2)}, u32[]{:S(2)}) collective-permute-start(bf16[128,1024]{1,0:T(8,128)(2,1)S(1)} %get-tuple-element.27), channel_id=1, source_target_pairs={{64,0},{66,2},{68,4},{70,6},{72,8},{74,10},{76,12},{78,14},{80,16}... | collective-permute-start | bytes 786440 | tf_op jit(solution)/shard_map/ppermute | solution.py:38
  88.2 5.4 %collective-permute-done.9 = bf16[128,1024]{1,0:T(8,128)(2,1)S(1)} collective-permute-done((bf16[128,1024]{1,0:T(8,128)(2,1)S(1)}, bf16[128,1024]{1,0:T(8,128)(2,1)S(1)}, u32[]{:S(2)}, u32[]{:S(2)}) %collective-permute-start.9) | collective-permute-done | bytes 262176 | tf_op jit(solution)/shard_map/ppermute | solution.py:38
  93.6 2.2 %collective-permute-done.10 = bf16[128,1024]{1,0:T(8,128)(2,1)S(1)} collective-permute-done((bf16[128,1024]{1,0:T(8,128)(2,1)S(1)}, bf16[128,1024]{1,0:T(8,128)(2,1)S(1)}, u32[]{:S(2)}, u32[]{:S(2)}) %collective-permute-start.10) | collective-permute-done | bytes 262176 | tf_op jit(solution)/shard_map/ppermute | solution.py:38
  95.9 0.9 collective-permute-done.11
  96.8 0.9 add_convert_fusion
  (29 shorter events, 4.4 us)
Async XLA Ops:
  2.2 6.0 %collective-permute-start.3 = (bf16[64,512]{1,0:T(8,128)(2,1)}, bf16[64,512]{1,0:T(8,128)(2,1)S(1)}, u32[]{:S(2)}, u32[]{:S(2)}) collective-permute-start(bf16[64,512]{1,0:T(8,128)(2,1)} %get-tuple-element.21), channel_id=1, source_target_pairs={{0,1},{1,0},{2,3},{3,2},{4,5},{5,4},{6,7},{7,6},{8,9},{9,8},{10,11... | collective-permute-start | bytes 196616 | tf_op jit(solution)/shard_map/ppermute | solution.py:42
  8.1 0.6 copy-start.3
  10.3 28.0 %copy-start.2 = (bf16[144,512]{1,0:T(8,128)(2,1)S(1)}, bf16[144,512]{1,0:T(8,128)(2,1)}, u32[]{:S(2)}) copy-start(bf16[144,512]{1,0:T(8,128)(2,1)} %shard_map.105.refs_3_.refs_4_) | copy-start | bytes 442372
  10.3 13.3 %collective-permute-start.5 = (bf16[144,512]{1,0:T(8,128)(2,1)}, bf16[144,512]{1,0:T(8,128)(2,1)S(1)}, u32[]{:S(2)}, u32[]{:S(2)}) collective-permute-start(bf16[144,512]{1,0:T(8,128)(2,1)} %shard_map.105.refs_3_.refs_4_), channel_id=1, source_target_pairs={{56,0},{58,2},{60,4},{62,6},{0,8},{2,10},{4,12},{6,14},{8,16},{10,... | collective-permute-start | bytes 442376 | tf_op jit(solution)/shard_map/ppermute | solution.py:38
  12.2 15.9 %collective-permute-start.4 = (bf16[144,512]{1,0:T(8,128)(2,1)}, bf16[144,512]{1,0:T(8,128)(2,1)S(1)}, u32[]{:S(2)}, u32[]{:S(2)}) collective-permute-start(bf16[144,512]{1,0:T(8,128)(2,1)} %shard_map.105.refs_3_.refs_4_), channel_id=1, source_target_pairs={{8,0},{10,2},{12,4},{14,6},{16,8},{18,10},{20,12},{22,14},{24,16},... | collective-permute-start | bytes 442376 | tf_op jit(solution)/shard_map/ppermute | solution.py:38
  18.4 28.0 %copy-start.1 = (bf16[272,1024]{1,0:T(8,128)(2,1)S(1)}, bf16[272,1024]{1,0:T(8,128)(2,1)}, u32[]{:S(2)}) copy-start(bf16[272,1024]{1,0:T(8,128)(2,1)} %shard_map.103.refs_0_) | copy-start | bytes 1671172
  18.4 19.9 %collective-permute-start.1 = (bf16[272,1024]{1,0:T(8,128)(2,1)}, bf16[272,1024]{1,0:T(8,128)(2,1)S(1)}, u32[]{:S(2)}, u32[]{:S(2)}) collective-permute-start(bf16[272,1024]{1,0:T(8,128)(2,1)} %shard_map.103.refs_0_), channel_id=1, source_target_pairs={{192,0},{194,2},{196,4},{198,6},{200,8},{202,10},{204,12},{206,14}... | collective-permute-start | bytes 1671176 | tf_op jit(solution)/shard_map/ppermute | solution.py:38
  20.0 18.3 %collective-permute-start = (bf16[272,1024]{1,0:T(8,128)(2,1)}, bf16[272,1024]{1,0:T(8,128)(2,1)S(1)}, u32[]{:S(2)}, u32[]{:S(2)}) collective-permute-start(bf16[272,1024]{1,0:T(8,128)(2,1)} %shard_map.103.refs_0_), channel_id=1, source_target_pairs={{64,0},{66,2},{68,4},{70,6},{72,8},{74,10},{76,12},{78,14},{80,16}... | collective-permute-start | bytes 1671176 | tf_op jit(solution)/shard_map/ppermute | solution.py:38
  21.6 24.8 %collective-permute-start.2 = (bf16[272,1024]{1,0:T(8,128)(2,1)}, bf16[272,1024]{1,0:T(8,128)(2,1)S(1)}, u32[]{:S(2)}, u32[]{:S(2)}) collective-permute-start(bf16[272,1024]{1,0:T(8,128)(2,1)} %shard_map.103.refs_0_), channel_id=1, source_target_pairs={{128,0},{130,2},{132,4},{134,6},{136,8},{138,10},{140,12},{142,14}... | collective-permute-start | bytes 1671176 | tf_op jit(solution)/shard_map/ppermute | solution.py:38
  23.6 13.2 %collective-permute-start.6 = (bf16[144,512]{1,0:T(8,128)(2,1)}, bf16[144,512]{1,0:T(8,128)(2,1)S(1)}, u32[]{:S(2)}, u32[]{:S(2)}) collective-permute-start(bf16[144,512]{1,0:T(8,128)(2,1)} %shard_map.105.refs_3_.refs_4_), channel_id=1, source_target_pairs={{32,0},{34,2},{36,4},{38,6},{40,8},{42,10},{44,12},{46,14},{48,16}... | collective-permute-start | bytes 442376 | tf_op jit(solution)/shard_map/ppermute | solution.py:38
  29.2 13.7 %collective-permute-start.8 = (bf16[288,512]{1,0:T(8,128)(2,1)S(1)}, bf16[288,512]{1,0:T(8,128)(2,1)S(1)}, u32[]{:S(2)}, u32[]{:S(2)}) collective-permute-start(bf16[288,512]{1,0:T(8,128)(2,1)S(1)} %get-tuple-element.39), channel_id=1, source_target_pairs={{48,0},{50,2},{52,4},{54,6},{56,8},{58,10},{60,12},{62,14},{0,16},... | collective-permute-start | bytes 884744 | tf_op jit(solution)/shard_map/ppermute | solution.py:38
  36.8 9.6 %collective-permute-start.7 = (bf16[288,512]{1,0:T(8,128)(2,1)S(1)}, bf16[288,512]{1,0:T(8,128)(2,1)S(1)}, u32[]{:S(2)}, u32[]{:S(2)}) collective-permute-start(bf16[288,512]{1,0:T(8,128)(2,1)S(1)} %get-tuple-element.40), channel_id=1, source_target_pairs={{16,0},{18,2},{20,4},{22,6},{24,8},{26,10},{28,12},{30,14},{32,16}... | collective-permute-start | bytes 884744 | tf_op jit(solution)/shard_map/ppermute | solution.py:38
  38.3 1.1 %copy-start = (bf16[272,1024]{1,0:T(8,128)(2,1)S(1)}, bf16[272,1024]{1,0:T(8,128)(2,1)}, u32[]{:S(2)}) copy-start(bf16[272,1024]{1,0:T(8,128)(2,1)} %shard_map.103.refs_0_) | copy-start | bytes 1671172
  49.4 12.3 %collective-permute-start.12 = (bf16[128,512]{1,0:T(8,128)(2,1)S(1)}, bf16[128,512]{1,0:T(8,128)(2,1)S(1)}, u32[]{:S(2)}, u32[]{:S(2)}) collective-permute-start(bf16[128,512]{1,0:T(8,128)(2,1)S(1)} %get-tuple-element.30), channel_id=1, source_target_pairs={{56,0},{58,2},{60,4},{62,6},{0,8},{2,10},{4,12},{6,14},{8,16},{10,... | collective-permute-start | bytes 393224 | tf_op jit(solution)/shard_map/ppermute | solution.py:38
  53.3 12.6 %collective-permute-start.13 = (bf16[128,512]{1,0:T(8,128)(2,1)S(1)}, bf16[128,512]{1,0:T(8,128)(2,1)S(1)}, u32[]{:S(2)}, u32[]{:S(2)}) collective-permute-start(bf16[128,512]{1,0:T(8,128)(2,1)S(1)} %get-tuple-element.31), channel_id=1, source_target_pairs={{8,0},{10,2},{12,4},{14,6},{16,8},{18,10},{20,12},{22,14},{24,16},... | collective-permute-start | bytes 393224 | tf_op jit(solution)/shard_map/ppermute | solution.py:38
  56.7 13.4 %collective-permute-start.14 = (bf16[128,512]{1,0:T(8,128)(2,1)S(1)}, bf16[128,512]{1,0:T(8,128)(2,1)S(1)}, u32[]{:S(2)}, u32[]{:S(2)}) collective-permute-start(bf16[128,512]{1,0:T(8,128)(2,1)S(1)} %get-tuple-element.32), channel_id=1, source_target_pairs={{32,0},{34,2},{36,4},{38,6},{40,8},{42,10},{44,12},{46,14},{48,16}... | collective-permute-start | bytes 393224 | tf_op jit(solution)/shard_map/ppermute | solution.py:38
  57.5 21.2 %collective-permute-start.15 = (bf16[128,512]{1,0:T(8,128)(2,1)S(1)}, bf16[128,512]{1,0:T(8,128)(2,1)S(1)}, u32[]{:S(2)}, u32[]{:S(2)}) collective-permute-start(bf16[128,512]{1,0:T(8,128)(2,1)S(1)} %get-tuple-element.33), channel_id=1, source_target_pairs={{48,0},{50,2},{52,4},{54,6},{56,8},{58,10},{60,12},{62,14},{0,16},... | collective-permute-start | bytes 393224 | tf_op jit(solution)/shard_map/ppermute | solution.py:38
  60.3 18.4 %collective-permute-start.16 = (bf16[128,512]{1,0:T(8,128)(2,1)S(1)}, bf16[128,512]{1,0:T(8,128)(2,1)S(1)}, u32[]{:S(2)}, u32[]{:S(2)}) collective-permute-start(bf16[128,512]{1,0:T(8,128)(2,1)S(1)} %get-tuple-element.34), channel_id=1, source_target_pairs={{40,0},{42,2},{44,4},{46,6},{48,8},{50,10},{52,12},{54,14},{56,16}... | collective-permute-start | bytes 393224 | tf_op jit(solution)/shard_map/ppermute | solution.py:38
  61.7 16.9 %collective-permute-start.17 = (bf16[128,512]{1,0:T(8,128)(2,1)S(1)}, bf16[128,512]{1,0:T(8,128)(2,1)S(1)}, u32[]{:S(2)}, u32[]{:S(2)}) collective-permute-start(bf16[128,512]{1,0:T(8,128)(2,1)S(1)} %get-tuple-element.35), channel_id=1, source_target_pairs={{16,0},{18,2},{20,4},{22,6},{24,8},{26,10},{28,12},{30,14},{32,16}... | collective-permute-start | bytes 393224 | tf_op jit(solution)/shard_map/ppermute | solution.py:38
  65.9 15.0 %collective-permute-start.18 = (bf16[128,512]{1,0:T(8,128)(2,1)S(1)}, bf16[128,512]{1,0:T(8,128)(2,1)S(1)}, u32[]{:S(2)}, u32[]{:S(2)}) collective-permute-start(bf16[128,512]{1,0:T(8,128)(2,1)S(1)} %get-tuple-element.36), channel_id=1, source_target_pairs={{24,0},{26,2},{28,4},{30,6},{32,8},{34,10},{36,12},{38,14},{40,16}... | collective-permute-start | bytes 393224 | tf_op jit(solution)/shard_map/ppermute | solution.py:38
  81.0 5.9 %collective-permute-start.19 = (bf16[64,512]{1,0:T(8,128)(2,1)S(1)}, bf16[64,512]{1,0:T(8,128)(2,1)S(1)}, u32[]{:S(2)}, u32[]{:S(2)}) collective-permute-start(bf16[64,512]{1,0:T(8,128)(2,1)S(1)} %broadcast_select_fusion.2), channel_id=1, source_target_pairs={{0,1},{1,0},{2,3},{3,2},{4,5},{5,4},{6,7},{7,6},{8,9},{9,8},{10,11... | collective-permute-start | bytes 196616 | tf_op jit(solution)/shard_map/ppermute | solution.py:42
  83.3 10.4 %collective-permute-start.9 = (bf16[128,1024]{1,0:T(8,128)(2,1)S(1)}, bf16[128,1024]{1,0:T(8,128)(2,1)S(1)}, u32[]{:S(2)}, u32[]{:S(2)}) collective-permute-start(bf16[128,1024]{1,0:T(8,128)(2,1)S(1)} %get-tuple-element.26), channel_id=1, source_target_pairs={{192,0},{194,2},{196,4},{198,6},{200,8},{202,10},{204,12},{206,14}... | collective-permute-start | bytes 786440 | tf_op jit(solution)/shard_map/ppermute | solution.py:38
  83.3 12.6 %collective-permute-start.10 = (bf16[128,1024]{1,0:T(8,128)(2,1)S(1)}, bf16[128,1024]{1,0:T(8,128)(2,1)S(1)}, u32[]{:S(2)}, u32[]{:S(2)}) collective-permute-start(bf16[128,1024]{1,0:T(8,128)(2,1)S(1)} %get-tuple-element.27), channel_id=1, source_target_pairs={{64,0},{66,2},{68,4},{70,6},{72,8},{74,10},{76,12},{78,14},{80,16}... | collective-permute-start | bytes 786440 | tf_op jit(solution)/shard_map/ppermute | solution.py:38
  86.5 10.3 %collective-permute-start.11 = (bf16[128,1024]{1,0:T(8,128)(2,1)S(1)}, bf16[128,1024]{1,0:T(8,128)(2,1)S(1)}, u32[]{:S(2)}, u32[]{:S(2)}) collective-permute-start(bf16[128,1024]{1,0:T(8,128)(2,1)S(1)} %get-tuple-element.28), channel_id=1, source_target_pairs={{128,0},{130,2},{132,4},{134,6},{136,8},{138,10},{140,12},{142,14}... | collective-permute-start | bytes 786440 | tf_op jit(solution)/shard_map/ppermute | solution.py:38
where the time goes:
time: 99.3 us; the launch traced here: 97.7 us
  starting transfers between devices  42.6 us (43%)
  waiting for transfers between devices  37.5 us (38%)
  Pallas kernels  11.8 us (12%)
  other arithmetic  3.28 us (3%)
  local copies, waits for them, and re-layouts  1.69 us (2%)
    ppermute x18, starting transfers between devices, shifted(): return lax.ppermute(value, 'ctx', pairs)  38.3 us
    ppermute x18, waiting for transfers between devices, shifted(): return lax.ppermute(value, 'ctx', pairs)  33.7 us
    pallas_call x2, Pallas kernels, call_grads(): pl.pallas_call(body, out_shape=out_shape, in_specs=[VMEM_SPEC] * len(oper...  6.52 us
    ppermute x2, starting transfers between devices, swap_head(): return lax.ppermute(value, 'head', [(0, 1), (1, 0)])  4.34 us
    ppermute x2, waiting for transfers between devices, swap_head(): return lax.ppermute(value, 'head', [(0, 1), (1, 0)])  3.88 us
    pallas_call x1, Pallas kernels, shards(): pl.pallas_call(pack_rows_kernel, out_shape=shape((2 * rows + AUX, width),...  2.19 us
  transfers between devices with their start and end apart: 20, of which 9 were waited for; matrix products, arithmetic and copies ran while one was open for 2% of the time, Pallas kernels for 6%

commit v1 on v0

--- a/solution.py
+++ b/solution.py
@@ -14,7 +14,7 @@
 GRID_Y = 4
 GRID_Z = 8
 ROW_SHIFTS = (0, 1, -1, 2)
-AUX = 16
+AUX = 8
 LOG2E = math.log2(math.e)
 SCALE = HEAD_DIM ** (-0.5)
 
@@ -76,62 +76,24 @@
             out_ref[base + 3 + at : base + 4 + at, span] = part
 
 
-def pick_kernel(head_ref, k_ref, v_ref, keep_ref, send_ref):
-    width = k_ref.shape[1] // 2
-    head = head_ref[0]
-
-    def fill(mine, other):
-        keep_ref[:, :width] = k_ref[:, mine * width : (mine + 1) * width]
-        keep_ref[:, width:] = v_ref[:, mine * width : (mine + 1) * width]
-        send_ref[:, :width] = k_ref[:, other * width : (other + 1) * width]
-        send_ref[:, width:] = v_ref[:, other * width : (other + 1) * width]
-
-    pl.when(head == 0)(lambda: fill(0, 1))
-    pl.when(head != 0)(lambda: fill(1, 0))
-
-
-def pack_cols_kernel(head_ref, keep_ref, got_ref, order_ref, out_ref):
-    half, width = keep_ref.shape
-    head = head_ref[0]
-
-    @pl.when(head == 0)
-    def _():
-        out_ref[0:half, :] = keep_ref[...]
-        out_ref[half : 2 * half, :] = got_ref[...]
-
-    @pl.when(head != 0)
-    def _():
-        out_ref[0:half, :] = got_ref[...]
-        out_ref[half : 2 * half, :] = keep_ref[...]
-
-    base = 2 * half
-    out_ref[base : base + AUX, :] = jnp.zeros((AUX, width), jnp.bfloat16)
-    for at, part in enumerate(split_place(order_ref[...])):
-        out_ref[base : base + 1, at * 2 * half : (at + 1) * 2 * half] = part
-
-
-def grads_kernel(n_rows, col_places, done_rows, done_cols, given, final, *refs):
+def grads_kernel(row_places, col_places, dq_given, kv_given, dq_final, kv_final, *refs):
+    n_rows = len(row_places)
     n_cols = len(col_places)
-    n_col_refs = 1 + max(at for at, _ in col_places)
     refs = list(refs)
 
     def take(count):
         taken, refs[:] = refs[:count], refs[count:]
         return taken
 
-    row_refs = take(n_rows)
-    col_refs = take(n_col_refs)
-    sums_in = take(3) if given else None
-    if final:
-        dq_refs = take(n_rows)
-        dkv_refs = take(n_cols)
-    else:
-        sums_out = take(3)
+    row_refs = take(1 + max(at for place in row_places for at, _ in place))
+    col_refs = take(1 + max(at for at, _ in col_places))
+    dq_in = take(dq_given)
+    kv_in = take(2 * kv_given)
+    dq_refs = take(n_rows if dq_final else 1)
+    dkv_refs = take(n_cols if kv_final else 2)
     qs, gs, lse_s, dot_s, first_s, last_s, ks, vs, kts = take(9)
-    if final:
-        dqt, dk, dv = take(3)
-    else:
-        dqt, dk, dv = sums_out
+    dqt = take(1)[0] if dq_final else dq_refs[0]
+    dk, dv = take(2) if kv_final else dkv_refs
     starts, listed, counts = take(3)
     rows = 128
     heads = row_refs[0].shape[1] // HEAD_DIM
@@ -155,13 +117,12 @@
         place = (aux[0:1, 0:rows] * 128.0 + aux[0:1, rows : 2 * rows]).astype(jnp.int32)
         col_starts.append(jnp.min(place))
         starts[c] = col_starts[-1]
-    for r, ref in enumerate(row_refs):
-        base = 2 * rows
+    for r, ((q_at, q_base), (g_at, g_base), (at, base)) in enumerate(row_places):
         for h in range(heads):
             span = slice(h * HEAD_DIM, (h + 1) * HEAD_DIM)
-            qs[r, span, :] = ref[0:rows, span]
-            gs[r, span, :] = ref[rows : 2 * rows, span]
-        aux = ref[base : base + AUX, :].astype(jnp.float32)
+            qs[r, span, :] = row_refs[q_at][q_base : q_base + rows, span]
+            gs[r, span, :] = row_refs[g_at][g_base : g_base + rows, span]
+        aux = row_refs[at][base : base + AUX, :].astype(jnp.float32)
         lse = (aux[0:1] + aux[1:2]) + aux[2:3]
         out_dot = (aux[3:4] + aux[4:5]) + aux[5:6]
         lse_s[r] = lse * LOG2E
@@ -177,19 +138,20 @@
         least = jnp.min(first)
         count = jnp.int32(0)
         for c in range(n_cols):
-            if r < done_rows and c < done_cols:
-                continue
             listed[r, count] = c
             some = (col_starts[c] <= most) & (col_starts[c] + (rows - 1) >= least)
             count = count + some.astype(jnp.int32)
         counts[r] = count
-    if given:
-        for old, new in zip(sums_in, (dqt, dk, dv)):
-            have = old.shape[0]
-            new[0:have] = old[...]
-            new[have:] = jnp.zeros((new.shape[0] - have,) + new.shape[1:], jnp.float32)
+    filled = 0
+    for old in dq_in:
+        dqt[filled : filled + old.shape[0]] = old[...]
+        filled += old.shape[0]
+    if filled == 0:
+        dqt[...] = jnp.zeros_like(dqt)
+    if kv_given:
+        dk[...] = kv_in[0][...]
+        dv[...] = kv_in[1][...]
     else:
-        dqt[...] = jnp.zeros_like(dqt)
         dk[...] = jnp.zeros_like(dk)
         dv[...] = jnp.zeros_like(dv)
 
@@ -243,13 +205,11 @@
 
     lax.fori_loop(0, n_rows, row_block, 0)
 
-    if not final:
-        return
-    for c, ref in enumerate(dkv_refs):
+    for c, ref in enumerate(dkv_refs if kv_final else ()):
         for j in range(kv_heads):
             ref[:, j * HEAD_DIM : (j + 1) * HEAD_DIM] = dk[c, j].astype(jnp.bfloat16)
             ref[:, (kv_heads + j) * HEAD_DIM : (kv_heads + j + 1) * HEAD_DIM] = dv[c, j].astype(jnp.bfloat16)
-    for r, ref in enumerate(dq_refs):
+    for r, ref in enumerate(dq_refs if dq_final else ()):
         for j in range(kv_heads):
             for g in range(group):
                 part = dqt[r, j, :, g * rows : (g + 1) * rows].astype(jnp.bfloat16)
@@ -257,23 +217,24 @@
                 ref[:, h * HEAD_DIM : (h + 1) * HEAD_DIM] = dot(eye, part, NT).astype(jnp.bfloat16)
 
 
-def call_grads(row_packs, col_packs, col_places, done, sums, final, rows, width, kv_width):
-    n_rows, n_cols = len(row_packs), len(col_places)
-    kv_heads = kv_width // HEAD_DIM
+def call_grads(row_packs, row_places, col_packs, col_places, dq_in, kv_in, dq_final, kv_final):
+    rows = 128
+    n_rows, n_cols = len(row_places), len(col_places)
+    width, all_kv = row_packs[0].shape[1], col_packs[0].shape[1]
+    kv_heads = all_kv // HEAD_DIM // 2
     heads = width // HEAD_DIM
     wide = heads // kv_heads * rows
     shape = jax.ShapeDtypeStruct
-    sum_shapes = (
-        (n_rows, kv_heads, HEAD_DIM, wide),
-        (n_cols, kv_heads, rows, HEAD_DIM),
-        (n_cols, kv_heads, rows, HEAD_DIM),
-    )
-    if final:
+    dq_shape = (n_rows, kv_heads, HEAD_DIM, wide)
+    kv_shape = (n_cols, kv_heads, rows, HEAD_DIM)
+    out_shape = (shape(dq_shape, jnp.float32),)
+    if dq_final:
         out_shape = (shape((rows, width), jnp.bfloat16),) * n_rows
-        out_shape += (shape((rows, 2 * kv_width), jnp.bfloat16),) * n_cols
+    if kv_final:
+        out_shape += (shape((rows, all_kv), jnp.bfloat16),) * n_cols
     else:
-        out_shape = tuple(shape(s, jnp.float32) for s in sum_shapes)
-    operands = (*row_packs, *col_packs, *sums)
+        out_shape += (shape(kv_shape, jnp.float32),) * 2
+    operands = (*row_packs, *col_packs, *dq_in, *kv_in)
     scratch = [
         pltpu.VMEM((n_rows, heads * rows, HEAD_DIM), jnp.bfloat16),
         pltpu.VMEM((n_rows, heads * rows, HEAD_DIM), jnp.bfloat16),
@@ -285,15 +246,19 @@
         pltpu.VMEM((n_cols, kv_heads, rows, HEAD_DIM), jnp.bfloat16),
         pltpu.VMEM((n_cols, kv_heads, HEAD_DIM, rows), jnp.bfloat16),
     ]
-    if final:
-        scratch += [pltpu.VMEM(s, jnp.float32) for s in sum_shapes]
+    if dq_final:
+        scratch += [pltpu.VMEM(dq_shape, jnp.float32)]
+    if kv_final:
+        scratch += [pltpu.VMEM(kv_shape, jnp.float32)] * 2
     scratch += [
         pltpu.SMEM((n_cols,), jnp.int32),
         pltpu.SMEM((n_rows, n_cols + 1), jnp.int32),
         pltpu.SMEM((n_rows,), jnp.int32),
     ]
-    body = functools.partial(grads_kernel, n_rows, col_places, *done, bool(sums), final)
-    return pl.pallas_call(
+    body = functools.partial(
+        grads_kernel, row_places, col_places, len(dq_in), bool(kv_in), dq_final, kv_final
+    )
+    outs = pl.pallas_call(
         body,
         out_shape=out_shape,
         in_specs=[VMEM_SPEC] * len(operands),
@@ -301,6 +266,8 @@
         scratch_shapes=scratch,
         compiler_params=pltpu.CompilerParams(vmem_limit_bytes=40 * 1024 * 1024),
     )(*operands)
+    cut = n_rows if dq_final else 1
+    return outs[:cut], outs[cut:]
 
 
 def shards(queries, key_states, value_states, attn_out, grad_out, log_sum_exp, token_order, position):
@@ -311,57 +278,59 @@
     order = token_order[None]
     shape = jax.ShapeDtypeStruct
 
-    keep, send = pl.pallas_call(
-        pick_kernel,
-        out_shape=(shape((half, 2 * kv_width), jnp.bfloat16),) * 2,
-        in_specs=[SMEM_SPEC, VMEM_SPEC, VMEM_SPEC],
-        out_specs=(VMEM_SPEC,) * 2,
-    )(head, key_states, value_states)
-    got = swap_head(send)
+    is_first = head[0] == 0
+    lower = jnp.concatenate([key_states[:, :kv_width], value_states[:, :kv_width]], axis=1)
+    upper = jnp.concatenate([key_states[:, kv_width:], value_states[:, kv_width:]], axis=1)
+    got = swap_head(jnp.where(is_first, upper, lower))
     row_pack = pl.pallas_call(
         pack_rows_kernel,
         out_shape=shape((2 * rows + AUX, width), jnp.bfloat16),
         in_specs=[VMEM_SPEC] * 6,
         out_specs=VMEM_SPEC,
     )(queries, attn_out, grad_out, log_sum_exp, order, position[None])
-    col_pack = pl.pallas_call(
-        pack_cols_kernel,
-        out_shape=shape((2 * half + AUX, 2 * kv_width), jnp.bfloat16),
-        in_specs=[SMEM_SPEC, VMEM_SPEC, VMEM_SPEC, VMEM_SPEC],
-        out_specs=VMEM_SPEC,
-    )(head, keep, got, order)
-
-    row_packs = [row_pack]
-    for s in (1, -1, 2):
-        row_packs.append(shifted(row_pack, s, 0))
+    keep = jnp.where(is_first, lower, upper)
+    places = jnp.concatenate([*split_place(token_order), jnp.zeros((2 * kv_width - 2 * rows,), jnp.bfloat16)])
+    col_pack = jnp.concatenate(
+        [
+            jnp.where(is_first, keep, got),
+            jnp.where(is_first, got, keep),
+            jnp.broadcast_to(places[None], (AUX, 2 * kv_width)),
+        ],
+        axis=0,
+    )
+
+    row_ahead = shifted(row_pack, 1, 0)
+    row_behind = shifted(row_pack, -1, 0)
+    row_two_q = shifted(row_ahead[:rows], 1, 0)
+    row_two_g = shifted(row_behind[rows:], -1, 0)
     ahead = shifted(col_pack, 0, 1)
     behind = shifted(col_pack, 0, -1)
     across = shifted(col_pack, 0, 4)
     ahead_pair = shifted(jnp.concatenate([col_pack, ahead], axis=0), 0, 2)
     behind_pair = shifted(jnp.concatenate([col_pack, behind], axis=0), 0, -2)
+
     size = 2 * half + AUX
+    first_rows = [row_pack, row_ahead, row_behind]
+    first_places = tuple(((r, 0), (r, rows), (r, 2 * rows)) for r in range(3))
+    two_rows = [row_two_q, row_two_g]
+    near = [col_pack, ahead, behind, across]
     near_places = ((0, 0), (1, 0), (2, 0), (3, 0))
-    far_places = ((4, 0), (4, size), (5, 0), (5, size))
-    col_shifts = (0, 1, -1, 4, 2, 3, -2, -3)
-    near = [col_pack, ahead, behind, across]
-
-    sums = call_grads(row_packs[:3], near, near_places, (0, 0), (), False, rows, width, kv_width)
-    outs = call_grads(
-        row_packs,
-        near + [ahead_pair, behind_pair],
-        near_places + far_places,
-        (3, 4),
-        sums,
-        True,
-        rows,
-        width,
-        kv_width,
+    near_shifts = (0, 1, -1, 4)
+    far = [ahead_pair, behind_pair]
+    far_places = ((0, 0), (0, size), (1, 0), (1, size))
+    far_shifts = (2, 3, -2, -3)
+    two_place = ((0, 0), (1, 0), (1, rows))
+    last_place = ((3, 0), (4, 0), (4, rows))
+
+    dq_first, kv_near = call_grads(first_rows, first_places, near, near_places, (), (), False, False)
+    dq_two, near_parts = call_grads(two_rows, (two_place,), near, near_places, (), kv_near, False, True)
+    dq_parts, far_parts = call_grads(
+        first_rows + two_rows, first_places + (last_place,), far, far_places, (*dq_first, *dq_two), (), True, True
     )
-    n_rows = len(ROW_SHIFTS)
-    dq_parts, dkv_parts = outs[:n_rows], outs[n_rows:]
-
-    dkv = dkv_parts[0].astype(jnp.float32)
-    for s, part in list(zip(col_shifts, dkv_parts))[1:]:
+
+    parts = dict(zip(near_shifts + far_shifts, (*near_parts, *far_parts)))
+    dkv = parts.pop(0).astype(jnp.float32)
+    for s, part in parts.items():
         back = shifted(part, 0, -s)
         dkv = dkv + back.astype(jnp.float32)
     dq = dq_parts[0].astype(jnp.float32)
@@ -371,7 +340,6 @@
     grad_queries = dq.astype(jnp.bfloat16)
 
     dkv = dkv.astype(jnp.bfloat16)
-    is_first = head[0] == 0
     send_back = jnp.where(is_first, dkv[half:], dkv[:half])
     mine = jnp.where(is_first, dkv[:half], dkv[half:])
     other = swap_head(send_back)

time: 99.3 us -> 108 us (1.088)
  the two profiles are of different devices: /device:TPU:2 before, /device:TPU:96 now
where the time goes in v1:
time: 108 us
  starting transfers between devices  51.9 us (48%)
  waiting for transfers between devices  39.8 us (37%)
  Pallas kernels  11.8 us (11%)
  other arithmetic  2.44 us (2%)
    ppermute x19, starting transfers between devices, shifted(): return lax.ppermute(value, 'ctx', pairs)  45.7 us
    ppermute x19, waiting for transfers between devices, shifted(): return lax.ppermute(value, 'ctx', pairs)  37.1 us
    pallas_call x3, Pallas kernels, call_grads(): pl.pallas_call(body, out_shape=out_shape, in_specs=[VMEM_SPEC] * len(oper...  9.6 us
    ppermute x2, starting transfers between devices, swap_head(): return lax.ppermute(value, 'head', [(0, 1), (1, 0)])  6.22 us
    ppermute x2, waiting for transfers between devices, swap_head(): return lax.ppermute(value, 'head', [(0, 1), (1, 0)])  2.72 us
    pallas_call x1, Pallas kernels, shards(): pl.pallas_call(pack_rows_kernel, out_shape=shape((2 * rows + AUX, width),...  2.18 us
  transfers between devices with their start and end apart: 21, of which 11 were waited for; matrix products, arithmetic and copies ran while one was open for 2% of the time, Pallas kernels for 2%

profile of v1, /device:TPU:96, one launch (start us, length us, event | category | flops | bytes accessed | tf_op | source)
XLA Modules:
  0.0 107.7 jit_solution(15412904142436585712)
XLA Ops:
  0.6 2.2 %shard_map.103.refs_0_ = bf16[264,1024]{1,0:T(8,128)(2,1)} custom-call(bf16[128,1024]{1,0:T(8,128)(2,1)} %q_ref.1, bf16[128,1024]{1,0:T(8,128)(2,1)} %o_ref.1, bf16[128,1024]{1,0:T(8,128)(2,1)} %g_ref.1, f32[8,128]{1,0:T(8,128)} %lse_ref.1, s32[1,128]{1,0:T(1,128)} %bitcast.3, s32[1,128]{1,0:T(1,128)} %bitcast.2), custom_call_target="tpu_custom_call" | custom-call | tf_op jit(solution)/shard_map/pallas_call | solution.py:285
  2.8 3.0 %collective-permute-start = (bf16[264,1024]{1,0:T(8,128)(2,1)}, bf16[264,1024]{1,0:T(8,128)(2,1)S(1)}, u32[]{:S(2)}, u32[]{:S(2)}) collective-permute-start(bf16[264,1024]{1,0:T(8,128)(2,1)} %shard_map.103.refs_0_), channel_id=1, source_target_pairs={{64,0},{66,2},{68,4},{70,6},{72,8},{74,10},{76,12},{78,14},{80,16}... | collective-permute-start | bytes 1622024 | tf_op jit(solution)/shard_map/ppermute | solution.py:38
  5.8 0.9 fusion.2
  6.8 3.1 %collective-permute-start.4 = (bf16[64,512]{1,0:T(8,128)(2,1)S(1)}, bf16[64,512]{1,0:T(8,128)(2,1)S(1)}, u32[]{:S(2)}, u32[]{:S(2)}) collective-permute-start(bf16[64,512]{1,0:T(8,128)(2,1)S(1)} %broadcast_select_fusion.6), channel_id=1, source_target_pairs={{0,1},{1,0},{2,3},{3,2},{4,5},{5,4},{6,7},{7,6},{8,9},{9,8},{10,11... | collective-permute-start | bytes 196616 | tf_op jit(solution)/shard_map/ppermute | solution.py:42
  9.9 2.7 %collective-permute-done.4 = bf16[64,512]{1,0:T(8,128)(2,1)S(1)} collective-permute-done((bf16[64,512]{1,0:T(8,128)(2,1)S(1)}, bf16[64,512]{1,0:T(8,128)(2,1)S(1)}, u32[]{:S(2)}, u32[]{:S(2)}) %collective-permute-start.4) | collective-permute-done | bytes 65568 | tf_op jit(solution)/shard_map/ppermute | solution.py:42
  12.9 3.1 %collective-permute-start.7 = (bf16[136,512]{1,0:T(8,128)(2,1)S(1)}, bf16[136,512]{1,0:T(8,128)(2,1)S(1)}, u32[]{:S(2)}, u32[]{:S(2)}) collective-permute-start(bf16[136,512]{1,0:T(8,128)(2,1)S(1)} %pad_maximum_fusion.3.refs_3_.refs_2_), channel_id=1, source_target_pairs={{56,0},{58,2},{60,4},{62,6},{0,8},{2,10},{4,12},{6,14},{8,16},{10,... | collective-permute-start | bytes 417800 | tf_op jit(solution)/shard_map/ppermute | solution.py:38
  16.0 5.0 %collective-permute-done.1.refs_2_ = bf16[264,1024]{1,0:T(8,128)(2,1)S(1)} collective-permute-done((bf16[264,1024]{1,0:T(8,128)(2,1)}, bf16[264,1024]{1,0:T(8,128)(2,1)S(1)}, u32[]{:S(2)}, u32[]{:S(2)}) %collective-permute-start.1) | collective-permute-done | bytes 540704 | tf_op jit(solution)/shard_map/ppermute | solution.py:38
  21.5 3.9 %collective-permute-start.8 = (bf16[272,512]{1,0:T(8,128)(2,1)S(1)}, bf16[272,512]{1,0:T(8,128)(2,1)S(1)}, u32[]{:S(2)}, u32[]{:S(2)}) collective-permute-start(bf16[272,512]{1,0:T(8,128)(2,1)S(1)} %get-tuple-element.39), channel_id=1, source_target_pairs={{48,0},{50,2},{52,4},{54,6},{56,8},{58,10},{60,12},{62,14},{0,16},... | collective-permute-start | bytes 835592 | tf_op jit(solution)/shard_map/ppermute | solution.py:38
  25.4 3.3 %collective-permute-start.2 = (bf16[128,1024]{1,0:T(8,128)(2,1)S(1)}, bf16[128,1024]{1,0:T(8,128)(2,1)S(1)}, u32[]{:S(2)}, u32[]{:S(2)}) collective-permute-start(bf16[128,1024]{1,0:T(8,128)(2,1)S(1)} %slice.50), channel_id=1, source_target_pairs={{64,0},{66,2},{68,4},{70,6},{72,8},{74,10},{76,12},{78,14},{80,16}... | collective-permute-start | bytes 786440 | tf_op jit(solution)/shard_map/ppermute | solution.py:38
  28.7 4.5 %collective-permute-start.9 = (bf16[136,512]{1,0:T(8,128)(2,1)S(1)}, bf16[136,512]{1,0:T(8,128)(2,1)S(1)}, u32[]{:S(2)}, u32[]{:S(2)}) collective-permute-start(bf16[136,512]{1,0:T(8,128)(2,1)S(1)} %pad_maximum_fusion.3.refs_3_.refs_2_), channel_id=1, source_target_pairs={{32,0},{34,2},{36,4},{38,6},{40,8},{42,10},{44,12},{46,14},{48,16}... | collective-permute-start | bytes 417800 | tf_op jit(solution)/shard_map/ppermute | solution.py:38
  33.2 9.0 %collective-permute-done.9.refs_6_.refs_5_ = bf16[136,512]{1,0:T(8,128)(2,1)S(1)} collective-permute-done((bf16[136,512]{1,0:T(8,128)(2,1)S(1)}, bf16[136,512]{1,0:T(8,128)(2,1)S(1)}, u32[]{:S(2)}, u32[]{:S(2)}) %collective-permute-start.9) | collective-permute-done | bytes 139296 | tf_op jit(solution)/shard_map/ppermute | solution.py:38
  42.2 1.7 %shard_map.104 = (f32[3,2,128,512]{3,2,1,0:T(8,128)S(1)}, f32[4,2,128,128]{3,2,1,0:T(8,128)S(1)}, f32[4,2,128,128]{3,2,1,0:T(8,128)S(1)}) custom-call(bf16[264,1024]{1,0:T(8,128)(2,1)S(1)} %copy-done, bf16[264,1024]{1,0:T(8,128)(2,1)S(1)} %collective-permute-done.refs_1_, bf16[264,1024]{1,0:T(8,128)(2,1)S(1)} %collective-permute-done.1.refs_2_, ...), custom_call_target="tpu_custom_call" | custom-call | tf_op jit(solution)/shard_map/pallas_call | solution.py:261
  43.9 0.7 shard_map.105
  44.6 7.2 %shard_map.106 = (bf16[128,1024]{1,0:T(8,128)(2,1)S(1)}, bf16[128,1024]{1,0:T(8,128)(2,1)S(1)}, bf16[128,1024]{1,0:T(8,128)(2,1)S(1)}, bf16[128,1024]{1,0:T(8,12...) custom-call(bf16[264,1024]{1,0:T(8,128)(2,1)S(1)} %copy-done, ...), custom_call_target="tpu_custom_call" | custom-call | tf_op jit(solution)/shard_map/pallas_call | solution.py:261
  51.8 5.0 %collective-permute-start.16 = (bf16[128,512]{1,0:T(8,128)(2,1)S(1)}, bf16[128,512]{1,0:T(8,128)(2,1)S(1)}, u32[]{:S(2)}, u32[]{:S(2)}) collective-permute-start(bf16[128,512]{1,0:T(8,128)(2,1)S(1)} %get-tuple-element.31), channel_id=1, source_target_pairs={{48,0},{50,2},{52,4},{54,6},{56,8},{58,10},{60,12},{62,14},{0,16},... | collective-permute-start | bytes 393224 | tf_op jit(solution)/shard_map/ppermute | solution.py:38
  56.8 1.6 %collective-permute-start.17 = (bf16[128,512]{1,0:T(8,128)(2,1)S(1)}, bf16[128,512]{1,0:T(8,128)(2,1)S(1)}, u32[]{:S(2)}, u32[]{:S(2)}) collective-permute-start(bf16[128,512]{1,0:T(8,128)(2,1)S(1)} %get-tuple-element.32), channel_id=1, source_target_pairs={{40,0},{42,2},{44,4},{46,6},{48,8},{50,10},{52,12},{54,14},{56,16}... | collective-permute-start | bytes 393224 | tf_op jit(solution)/shard_map/ppermute | solution.py:38
  58.4 2.8 %collective-permute-start.18 = (bf16[128,512]{1,0:T(8,128)(2,1)S(1)}, bf16[128,512]{1,0:T(8,128)(2,1)S(1)}, u32[]{:S(2)}, u32[]{:S(2)}) collective-permute-start(bf16[128,512]{1,0:T(8,128)(2,1)S(1)} %get-tuple-element.33), channel_id=1, source_target_pairs={{16,0},{18,2},{20,4},{22,6},{24,8},{26,10},{28,12},{30,14},{32,16}... | collective-permute-start | bytes 393224 | tf_op jit(solution)/shard_map/ppermute | solution.py:38
  61.3 4.5 %collective-permute-start.13 = (bf16[128,512]{1,0:T(8,128)(2,1)S(1)}, bf16[128,512]{1,0:T(8,128)(2,1)S(1)}, u32[]{:S(2)}, u32[]{:S(2)}) collective-permute-start(bf16[128,512]{1,0:T(8,128)(2,1)S(1)} %get-tuple-element.28), channel_id=1, source_target_pairs={{56,0},{58,2},{60,4},{62,6},{0,8},{2,10},{4,12},{6,14},{8,16},{10,... | collective-permute-start | bytes 393224 | tf_op jit(solution)/shard_map/ppermute | solution.py:38
  65.8 1.3 %collective-permute-done.16 = bf16[128,512]{1,0:T(8,128)(2,1)S(1)} collective-permute-done((bf16[128,512]{1,0:T(8,128)(2,1)S(1)}, bf16[128,512]{1,0:T(8,128)(2,1)S(1)}, u32[]{:S(2)}, u32[]{:S(2)}) %collective-permute-start.16) | collective-permute-done | bytes 131104 | tf_op jit(solution)/shard_map/ppermute | solution.py:38
  67.1 2.5 %collective-permute-start.14 = (bf16[128,512]{1,0:T(8,128)(2,1)S(1)}, bf16[128,512]{1,0:T(8,128)(2,1)S(1)}, u32[]{:S(2)}, u32[]{:S(2)}) collective-permute-start(bf16[128,512]{1,0:T(8,128)(2,1)S(1)} %get-tuple-element.29), channel_id=1, source_target_pairs={{8,0},{10,2},{12,4},{14,6},{16,8},{18,10},{20,12},{22,14},{24,16},... | collective-permute-start | bytes 393224 | tf_op jit(solution)/shard_map/ppermute | solution.py:38
  69.6 2.7 %collective-permute-done.17 = bf16[128,512]{1,0:T(8,128)(2,1)S(1)} collective-permute-done((bf16[128,512]{1,0:T(8,128)(2,1)S(1)}, bf16[128,512]{1,0:T(8,128)(2,1)S(1)}, u32[]{:S(2)}, u32[]{:S(2)}) %collective-permute-start.17) | collective-permute-done | bytes 131104 | tf_op jit(solution)/shard_map/ppermute | solution.py:38
  72.4 3.6 %collective-permute-done.19 = bf16[128,512]{1,0:T(8,128)(2,1)S(1)} collective-permute-done((bf16[128,512]{1,0:T(8,128)(2,1)S(1)}, bf16[128,512]{1,0:T(8,128)(2,1)S(1)}, u32[]{:S(2)}, u32[]{:S(2)}) %collective-permute-start.19) | collective-permute-done | bytes 131104 | tf_op jit(solution)/shard_map/ppermute | solution.py:38
  75.9 2.4 %collective-permute-done.14 = bf16[128,512]{1,0:T(8,128)(2,1)S(1)} collective-permute-done((bf16[128,512]{1,0:T(8,128)(2,1)S(1)}, bf16[128,512]{1,0:T(8,128)(2,1)S(1)}, u32[]{:S(2)}, u32[]{:S(2)}) %collective-permute-start.14) | collective-permute-done | bytes 131104 | tf_op jit(solution)/shard_map/ppermute | solution.py:38
  78.3 3.0 %collective-permute-done.15 = bf16[128,512]{1,0:T(8,128)(2,1)S(1)} collective-permute-done((bf16[128,512]{1,0:T(8,128)(2,1)S(1)}, bf16[128,512]{1,0:T(8,128)(2,1)S(1)}, u32[]{:S(2)}, u32[]{:S(2)}) %collective-permute-start.15) | collective-permute-done | bytes 131104 | tf_op jit(solution)/shard_map/ppermute | solution.py:38
  81.5 3.1 %collective-permute-start.20 = (bf16[64,512]{1,0:T(8,128)(2,1)S(1)}, bf16[64,512]{1,0:T(8,128)(2,1)S(1)}, u32[]{:S(2)}, u32[]{:S(2)}) collective-permute-start(bf16[64,512]{1,0:T(8,128)(2,1)S(1)} %broadcast_select_fusion.2), channel_id=1, source_target_pairs={{0,1},{1,0},{2,3},{3,2},{4,5},{5,4},{6,7},{7,6},{8,9},{9,8},{10,11... | collective-permute-start | bytes 196616 | tf_op jit(solution)/shard_map/ppermute | solution.py:42
  84.6 3.5 %collective-permute-start.10 = (bf16[128,1024]{1,0:T(8,128)(2,1)S(1)}, bf16[128,1024]{1,0:T(8,128)(2,1)S(1)}, u32[]{:S(2)}, u32[]{:S(2)}) collective-permute-start(bf16[128,1024]{1,0:T(8,128)(2,1)S(1)} %get-tuple-element.24), channel_id=1, source_target_pairs={{192,0},{194,2},{196,4},{198,6},{200,8},{202,10},{204,12},{206,14}... | collective-permute-start | bytes 786440 | tf_op jit(solution)/shard_map/ppermute | solution.py:38
  88.1 5.9 %collective-permute-start.11 = (bf16[128,1024]{1,0:T(8,128)(2,1)S(1)}, bf16[128,1024]{1,0:T(8,128)(2,1)S(1)}, u32[]{:S(2)}, u32[]{:S(2)}) collective-permute-start(bf16[128,1024]{1,0:T(8,128)(2,1)S(1)} %get-tuple-element.25), channel_id=1, source_target_pairs={{64,0},{66,2},{68,4},{70,6},{72,8},{74,10},{76,12},{78,14},{80,16}... | collective-permute-start | bytes 786440 | tf_op jit(solution)/shard_map/ppermute | solution.py:38
  94.0 1.5 %collective-permute-start.12 = (bf16[128,1024]{1,0:T(8,128)(2,1)S(1)}, bf16[128,1024]{1,0:T(8,128)(2,1)S(1)}, u32[]{:S(2)}, u32[]{:S(2)}) collective-permute-start(bf16[128,1024]{1,0:T(8,128)(2,1)S(1)} %get-tuple-element.26), channel_id=1, source_target_pairs={{128,0},{130,2},{132,4},{134,6},{136,8},{138,10},{140,12},{142,14}... | collective-permute-start | bytes 786440 | tf_op jit(solution)/shard_map/ppermute | solution.py:38
  96.8 3.5 %collective-permute-done.10 = bf16[128,1024]{1,0:T(8,128)(2,1)S(1)} collective-permute-done((bf16[128,1024]{1,0:T(8,128)(2,1)S(1)}, bf16[128,1024]{1,0:T(8,128)(2,1)S(1)}, u32[]{:S(2)}, u32[]{:S(2)}) %collective-permute-start.10) | collective-permute-done | bytes 262176 | tf_op jit(solution)/shard_map/ppermute | solution.py:38
  100.3 4.7 %collective-permute-done.11 = bf16[128,1024]{1,0:T(8,128)(2,1)S(1)} collective-permute-done((bf16[128,1024]{1,0:T(8,128)(2,1)S(1)}, bf16[128,1024]{1,0:T(8,128)(2,1)S(1)}, u32[]{:S(2)}, u32[]{:S(2)}) %collective-permute-start.11) | collective-permute-done | bytes 262176 | tf_op jit(solution)/shard_map/ppermute | solution.py:38
  104.9 1.9 %collective-permute-done.12 = bf16[128,1024]{1,0:T(8,128)(2,1)S(1)} collective-permute-done((bf16[128,1024]{1,0:T(8,128)(2,1)S(1)}, bf16[128,1024]{1,0:T(8,128)(2,1)S(1)}, u32[]{:S(2)}, u32[]{:S(2)}) %collective-permute-start.12) | collective-permute-done | bytes 262176 | tf_op jit(solution)/shard_map/ppermute | solution.py:38
  106.8 0.9 add_convert_fusion
  (37 shorter events, 2.3 us)
Async XLA Ops:
  0.6 9.2 %copy-start.1 = (s32[128]{0:T(128)S(1)}, s32[128]{0:T(128)}, u32[]{:S(2)}) copy-start(s32[128]{0:T(128)} %param.14) | copy-start | bytes 1540
  2.8 22.6 %collective-permute-start = (bf16[264,1024]{1,0:T(8,128)(2,1)}, bf16[264,1024]{1,0:T(8,128)(2,1)S(1)}, u32[]{:S(2)}, u32[]{:S(2)}) collective-permute-start(bf16[264,1024]{1,0:T(8,128)(2,1)} %shard_map.103.refs_0_), channel_id=1, source_target_pairs={{64,0},{66,2},{68,4},{70,6},{72,8},{74,10},{76,12},{78,14},{80,16}... | collective-permute-start | bytes 1622024 | tf_op jit(solution)/shard_map/ppermute | solution.py:38
  5.8 15.2 %collective-permute-start.1 = (bf16[264,1024]{1,0:T(8,128)(2,1)}, bf16[264,1024]{1,0:T(8,128)(2,1)S(1)}, u32[]{:S(2)}, u32[]{:S(2)}) collective-permute-start(bf16[264,1024]{1,0:T(8,128)(2,1)} %shard_map.103.refs_0_), channel_id=1, source_target_pairs={{192,0},{194,2},{196,4},{198,6},{200,8},{202,10},{204,12},{206,14}... | collective-permute-start | bytes 1622024 | tf_op jit(solution)/shard_map/ppermute | solution.py:38
  5.8 36.3 %copy-start = (bf16[264,1024]{1,0:T(8,128)(2,1)S(1)}, bf16[264,1024]{1,0:T(8,128)(2,1)}, u32[]{:S(2)}) copy-start(bf16[264,1024]{1,0:T(8,128)(2,1)} %shard_map.103.refs_0_) | copy-start | bytes 1622020
  6.8 5.9 %collective-permute-start.4 = (bf16[64,512]{1,0:T(8,128)(2,1)S(1)}, bf16[64,512]{1,0:T(8,128)(2,1)S(1)}, u32[]{:S(2)}, u32[]{:S(2)}) collective-permute-start(bf16[64,512]{1,0:T(8,128)(2,1)S(1)} %broadcast_select_fusion.6), channel_id=1, source_target_pairs={{0,1},{1,0},{2,3},{3,2},{4,5},{5,4},{6,7},{7,6},{8,9},{9,8},{10,11... | collective-permute-start | bytes 196616 | tf_op jit(solution)/shard_map/ppermute | solution.py:42
  12.7 8.4 %collective-permute-start.5 = (bf16[136,512]{1,0:T(8,128)(2,1)S(1)}, bf16[136,512]{1,0:T(8,128)(2,1)S(1)}, u32[]{:S(2)}, u32[]{:S(2)}) collective-permute-start(bf16[136,512]{1,0:T(8,128)(2,1)S(1)} %pad_maximum_fusion.3.refs_3_.refs_2_), channel_id=1, source_target_pairs={{8,0},{10,2},{12,4},{14,6},{16,8},{18,10},{20,12},{22,14},{24,16},... | collective-permute-start | bytes 417800 | tf_op jit(solution)/shard_map/ppermute | solution.py:38
  12.9 8.3 %collective-permute-start.7 = (bf16[136,512]{1,0:T(8,128)(2,1)S(1)}, bf16[136,512]{1,0:T(8,128)(2,1)S(1)}, u32[]{:S(2)}, u32[]{:S(2)}) collective-permute-start(bf16[136,512]{1,0:T(8,128)(2,1)S(1)} %pad_maximum_fusion.3.refs_3_.refs_2_), channel_id=1, source_target_pairs={{56,0},{58,2},{60,4},{62,6},{0,8},{2,10},{4,12},{6,14},{8,16},{10,... | collective-permute-start | bytes 417800 | tf_op jit(solution)/shard_map/ppermute | solution.py:38
  21.0 22.9 %collective-permute-start.3 = (bf16[136,1024]{1,0:T(8,128)(2,1)S(1)}, bf16[136,1024]{1,0:T(8,128)(2,1)S(1)}, u32[]{:S(2)}, u32[]{:S(2)}) collective-permute-start(bf16[136,1024]{1,0:T(8,128)(2,1)S(1)} %slice.51), channel_id=1, source_target_pairs={{192,0},{194,2},{196,4},{198,6},{200,8},{202,10},{204,12},{206,14}... | collective-permute-start | bytes 835592 | tf_op jit(solution)/shard_map/ppermute | solution.py:38
  21.2 23.4 %collective-permute-start.6 = (bf16[272,512]{1,0:T(8,128)(2,1)S(1)}, bf16[272,512]{1,0:T(8,128)(2,1)S(1)}, u32[]{:S(2)}, u32[]{:S(2)}) collective-permute-start(bf16[272,512]{1,0:T(8,128)(2,1)S(1)} %get-tuple-element.40), channel_id=1, source_target_pairs={{16,0},{18,2},{20,4},{22,6},{24,8},{26,10},{28,12},{30,14},{32,16}... | collective-permute-start | bytes 835592 | tf_op jit(solution)/shard_map/ppermute | solution.py:38
  21.5 23.0 %collective-permute-start.8 = (bf16[272,512]{1,0:T(8,128)(2,1)S(1)}, bf16[272,512]{1,0:T(8,128)(2,1)S(1)}, u32[]{:S(2)}, u32[]{:S(2)}) collective-permute-start(bf16[272,512]{1,0:T(8,128)(2,1)S(1)} %get-tuple-element.39), channel_id=1, source_target_pairs={{48,0},{50,2},{52,4},{54,6},{56,8},{58,10},{60,12},{62,14},{0,16},... | collective-permute-start | bytes 835592 | tf_op jit(solution)/shard_map/ppermute | solution.py:38
  25.4 18.4 %collective-permute-start.2 = (bf16[128,1024]{1,0:T(8,128)(2,1)S(1)}, bf16[128,1024]{1,0:T(8,128)(2,1)S(1)}, u32[]{:S(2)}, u32[]{:S(2)}) collective-permute-start(bf16[128,1024]{1,0:T(8,128)(2,1)S(1)} %slice.50), channel_id=1, source_target_pairs={{64,0},{66,2},{68,4},{70,6},{72,8},{74,10},{76,12},{78,14},{80,16}... | collective-permute-start | bytes 786440 | tf_op jit(solution)/shard_map/ppermute | solution.py:38
  28.7 13.5 %collective-permute-start.9 = (bf16[136,512]{1,0:T(8,128)(2,1)S(1)}, bf16[136,512]{1,0:T(8,128)(2,1)S(1)}, u32[]{:S(2)}, u32[]{:S(2)}) collective-permute-start(bf16[136,512]{1,0:T(8,128)(2,1)S(1)} %pad_maximum_fusion.3.refs_3_.refs_2_), channel_id=1, source_target_pairs={{32,0},{34,2},{36,4},{38,6},{40,8},{42,10},{44,12},{46,14},{48,16}... | collective-permute-start | bytes 417800 | tf_op jit(solution)/shard_map/ppermute | solution.py:38
  51.8 15.3 %collective-permute-start.16 = (bf16[128,512]{1,0:T(8,128)(2,1)S(1)}, bf16[128,512]{1,0:T(8,128)(2,1)S(1)}, u32[]{:S(2)}, u32[]{:S(2)}) collective-permute-start(bf16[128,512]{1,0:T(8,128)(2,1)S(1)} %get-tuple-element.31), channel_id=1, source_target_pairs={{48,0},{50,2},{52,4},{54,6},{56,8},{58,10},{60,12},{62,14},{0,16},... | collective-permute-start | bytes 393224 | tf_op jit(solution)/shard_map/ppermute | solution.py:38
  56.8 15.5 %collective-permute-start.17 = (bf16[128,512]{1,0:T(8,128)(2,1)S(1)}, bf16[128,512]{1,0:T(8,128)(2,1)S(1)}, u32[]{:S(2)}, u32[]{:S(2)}) collective-permute-start(bf16[128,512]{1,0:T(8,128)(2,1)S(1)} %get-tuple-element.32), channel_id=1, source_target_pairs={{40,0},{42,2},{44,4},{46,6},{48,8},{50,10},{52,12},{54,14},{56,16}... | collective-permute-start | bytes 393224 | tf_op jit(solution)/shard_map/ppermute | solution.py:38
  58.4 13.9 %collective-permute-start.18 = (bf16[128,512]{1,0:T(8,128)(2,1)S(1)}, bf16[128,512]{1,0:T(8,128)(2,1)S(1)}, u32[]{:S(2)}, u32[]{:S(2)}) collective-permute-start(bf16[128,512]{1,0:T(8,128)(2,1)S(1)} %get-tuple-element.33), channel_id=1, source_target_pairs={{16,0},{18,2},{20,4},{22,6},{24,8},{26,10},{28,12},{30,14},{32,16}... | collective-permute-start | bytes 393224 | tf_op jit(solution)/shard_map/ppermute | solution.py:38
  61.3 14.7 %collective-permute-start.19 = (bf16[128,512]{1,0:T(8,128)(2,1)S(1)}, bf16[128,512]{1,0:T(8,128)(2,1)S(1)}, u32[]{:S(2)}, u32[]{:S(2)}) collective-permute-start(bf16[128,512]{1,0:T(8,128)(2,1)S(1)} %get-tuple-element.34), channel_id=1, source_target_pairs={{24,0},{26,2},{28,4},{30,6},{32,8},{34,10},{36,12},{38,14},{40,16}... | collective-permute-start | bytes 393224 | tf_op jit(solution)/shard_map/ppermute | solution.py:38
  61.3 14.7 %collective-permute-start.13 = (bf16[128,512]{1,0:T(8,128)(2,1)S(1)}, bf16[128,512]{1,0:T(8,128)(2,1)S(1)}, u32[]{:S(2)}, u32[]{:S(2)}) collective-permute-start(bf16[128,512]{1,0:T(8,128)(2,1)S(1)} %get-tuple-element.28), channel_id=1, source_target_pairs={{56,0},{58,2},{60,4},{62,6},{0,8},{2,10},{4,12},{6,14},{8,16},{10,... | collective-permute-start | bytes 393224 | tf_op jit(solution)/shard_map/ppermute | solution.py:38
  67.1 11.2 %collective-permute-start.14 = (bf16[128,512]{1,0:T(8,128)(2,1)S(1)}, bf16[128,512]{1,0:T(8,128)(2,1)S(1)}, u32[]{:S(2)}, u32[]{:S(2)}) collective-permute-start(bf16[128,512]{1,0:T(8,128)(2,1)S(1)} %get-tuple-element.29), channel_id=1, source_target_pairs={{8,0},{10,2},{12,4},{14,6},{16,8},{18,10},{20,12},{22,14},{24,16},... | collective-permute-start | bytes 393224 | tf_op jit(solution)/shard_map/ppermute | solution.py:38
  72.3 9.0 %collective-permute-start.15 = (bf16[128,512]{1,0:T(8,128)(2,1)S(1)}, bf16[128,512]{1,0:T(8,128)(2,1)S(1)}, u32[]{:S(2)}, u32[]{:S(2)}) collective-permute-start(bf16[128,512]{1,0:T(8,128)(2,1)S(1)} %get-tuple-element.30), channel_id=1, source_target_pairs={{32,0},{34,2},{36,4},{38,6},{40,8},{42,10},{44,12},{46,14},{48,16}... | collective-permute-start | bytes 393224 | tf_op jit(solution)/shard_map/ppermute | solution.py:38
  81.5 14.0 %collective-permute-start.20 = (bf16[64,512]{1,0:T(8,128)(2,1)S(1)}, bf16[64,512]{1,0:T(8,128)(2,1)S(1)}, u32[]{:S(2)}, u32[]{:S(2)}) collective-permute-start(bf16[64,512]{1,0:T(8,128)(2,1)S(1)} %broadcast_select_fusion.2), channel_id=1, source_target_pairs={{0,1},{1,0},{2,3},{3,2},{4,5},{5,4},{6,7},{7,6},{8,9},{9,8},{10,11... | collective-permute-start | bytes 196616 | tf_op jit(solution)/shard_map/ppermute | solution.py:42
  84.6 15.7 %collective-permute-start.10 = (bf16[128,1024]{1,0:T(8,128)(2,1)S(1)}, bf16[128,1024]{1,0:T(8,128)(2,1)S(1)}, u32[]{:S(2)}, u32[]{:S(2)}) collective-permute-start(bf16[128,1024]{1,0:T(8,128)(2,1)S(1)} %get-tuple-element.24), channel_id=1, source_target_pairs={{192,0},{194,2},{196,4},{198,6},{200,8},{202,10},{204,12},{206,14}... | collective-permute-start | bytes 786440 | tf_op jit(solution)/shard_map/ppermute | solution.py:38
  88.1 16.8 %collective-permute-start.11 = (bf16[128,1024]{1,0:T(8,128)(2,1)S(1)}, bf16[128,1024]{1,0:T(8,128)(2,1)S(1)}, u32[]{:S(2)}, u32[]{:S(2)}) collective-permute-start(bf16[128,1024]{1,0:T(8,128)(2,1)S(1)} %get-tuple-element.25), channel_id=1, source_target_pairs={{64,0},{66,2},{68,4},{70,6},{72,8},{74,10},{76,12},{78,14},{80,16}... | collective-permute-start | bytes 786440 | tf_op jit(solution)/shard_map/ppermute | solution.py:38
  94.0 12.8 %collective-permute-start.12 = (bf16[128,1024]{1,0:T(8,128)(2,1)S(1)}, bf16[128,1024]{1,0:T(8,128)(2,1)S(1)}, u32[]{:S(2)}, u32[]{:S(2)}) collective-permute-start(bf16[128,1024]{1,0:T(8,128)(2,1)S(1)} %get-tuple-element.26), channel_id=1, source_target_pairs={{128,0},{130,2},{132,4},{134,6},{136,8},{138,10},{140,12},{142,14}... | collective-permute-start | bytes 786440 | tf_op jit(solution)/shard_map/ppermute | solution.py:38

commit v2 on v1

--- a/solution.py
+++ b/solution.py
@@ -313,12 +313,20 @@
     first_rows = [row_pack, row_ahead, row_behind]
     first_places = tuple(((r, 0), (r, rows), (r, 2 * rows)) for r in range(3))
     two_rows = [row_two_q, row_two_g]
-    near = [col_pack, ahead, behind, across]
-    near_places = ((0, 0), (1, 0), (2, 0), (3, 0))
-    near_shifts = (0, 1, -1, 4)
+    near = [col_pack, ahead, behind]
+    near_places = ((0, 0), (1, 0), (2, 0))
+    near_shifts = (0, 1, -1)
     far = [ahead_pair, behind_pair]
     far_places = ((0, 0), (0, size), (1, 0), (1, size))
     far_shifts = (2, 3, -2, -3)
+    if FOUR_NEAR:
+        near.append(across)
+        near_places += ((3, 0),)
+        near_shifts += (4,)
+    else:
+        far.append(across)
+        far_places += ((2, 0),)
+        far_shifts += (4,)
     two_place = ((0, 0), (1, 0), (1, rows))
     last_place = ((3, 0), (4, 0), (4, rows))
 
@@ -348,6 +356,9 @@
     grad_keys = jnp.concatenate([low[:, :kv_width], high[:, :kv_width]], axis=1)
     grad_values = jnp.concatenate([low[:, kv_width:], high[:, kv_width:]], axis=1)
     return grad_queries, grad_keys, grad_values
+
+
+FOUR_NEAR = True
 
 
 def solution(mesh):

time: 108 us -> 108 us (level)
  no operation moved by 1% of the time
where the time goes in v2:
time: 108 us
  starting transfers between devices  51.9 us (48%)
  waiting for transfers between devices  39.8 us (37%)
  Pallas kernels  11.8 us (11%)
  other arithmetic  2.44 us (2%)
    ppermute x19, starting transfers between devices, shifted(): return lax.ppermute(value, 'ctx', pairs)  45.7 us
    ppermute x19, waiting for transfers between devices, shifted(): return lax.ppermute(value, 'ctx', pairs)  37.1 us
    pallas_call x3, Pallas kernels, call_grads(): pl.pallas_call(body, out_shape=out_shape, in_specs=[VMEM_SPEC] * len(oper...  9.6 us
    ppermute x2, starting transfers between devices, swap_head(): return lax.ppermute(value, 'head', [(0, 1), (1, 0)])  6.22 us
    ppermute x2, waiting for transfers between devices, swap_head(): return lax.ppermute(value, 'head', [(0, 1), (1, 0)])  2.72 us
    pallas_call x1, Pallas kernels, shards(): pl.pallas_call(pack_rows_kernel, out_shape=shape((2 * rows + AUX, width),...  2.18 us
  transfers between devices with their start and end apart: 21, of which 11 were waited for; matrix products, arithmetic and copies ran while one was open for 2% of the time, Pallas kernels for 2%

profile of v2, /device:TPU:96, one launch (start us, length us, event | category | flops | bytes accessed | tf_op | source)
XLA Modules:
  0.0 107.7 jit_solution(15412904142436585712)
XLA Ops:
  0.6 2.2 %shard_map.103.refs_0_ = bf16[264,1024]{1,0:T(8,128)(2,1)} custom-call(bf16[128,1024]{1,0:T(8,128)(2,1)} %q_ref.1, bf16[128,1024]{1,0:T(8,128)(2,1)} %o_ref.1, bf16[128,1024]{1,0:T(8,128)(2,1)} %g_ref.1, f32[8,128]{1,0:T(8,128)} %lse_ref.1, s32[1,128]{1,0:T(1,128)} %bitcast.3, s32[1,128]{1,0:T(1,128)} %bitcast.2), custom_call_target="tpu_custom_call" | custom-call | tf_op jit(solution)/shard_map/pallas_call | solution.py:285
  2.8 3.0 %collective-permute-start = (bf16[264,1024]{1,0:T(8,128)(2,1)}, bf16[264,1024]{1,0:T(8,128)(2,1)S(1)}, u32[]{:S(2)}, u32[]{:S(2)}) collective-permute-start(bf16[264,1024]{1,0:T(8,128)(2,1)} %shard_map.103.refs_0_), channel_id=1, source_target_pairs={{64,0},{66,2},{68,4},{70,6},{72,8},{74,10},{76,12},{78,14},{80,16}... | collective-permute-start | bytes 1622024 | tf_op jit(solution)/shard_map/ppermute | solution.py:38
  5.8 0.9 fusion.2
  6.8 3.1 %collective-permute-start.4 = (bf16[64,512]{1,0:T(8,128)(2,1)S(1)}, bf16[64,512]{1,0:T(8,128)(2,1)S(1)}, u32[]{:S(2)}, u32[]{:S(2)}) collective-permute-start(bf16[64,512]{1,0:T(8,128)(2,1)S(1)} %broadcast_select_fusion.6), channel_id=1, source_target_pairs={{0,1},{1,0},{2,3},{3,2},{4,5},{5,4},{6,7},{7,6},{8,9},{9,8},{10,11... | collective-permute-start | bytes 196616 | tf_op jit(solution)/shard_map/ppermute | solution.py:42
  9.9 2.7 %collective-permute-done.4 = bf16[64,512]{1,0:T(8,128)(2,1)S(1)} collective-permute-done((bf16[64,512]{1,0:T(8,128)(2,1)S(1)}, bf16[64,512]{1,0:T(8,128)(2,1)S(1)}, u32[]{:S(2)}, u32[]{:S(2)}) %collective-permute-start.4) | collective-permute-done | bytes 65568 | tf_op jit(solution)/shard_map/ppermute | solution.py:42
  12.9 3.1 %collective-permute-start.7 = (bf16[136,512]{1,0:T(8,128)(2,1)S(1)}, bf16[136,512]{1,0:T(8,128)(2,1)S(1)}, u32[]{:S(2)}, u32[]{:S(2)}) collective-permute-start(bf16[136,512]{1,0:T(8,128)(2,1)S(1)} %pad_maximum_fusion.3.refs_3_.refs_2_), channel_id=1, source_target_pairs={{56,0},{58,2},{60,4},{62,6},{0,8},{2,10},{4,12},{6,14},{8,16},{10,... | collective-permute-start | bytes 417800 | tf_op jit(solution)/shard_map/ppermute | solution.py:38
  16.0 5.0 %collective-permute-done.1.refs_2_ = bf16[264,1024]{1,0:T(8,128)(2,1)S(1)} collective-permute-done((bf16[264,1024]{1,0:T(8,128)(2,1)}, bf16[264,1024]{1,0:T(8,128)(2,1)S(1)}, u32[]{:S(2)}, u32[]{:S(2)}) %collective-permute-start.1) | collective-permute-done | bytes 540704 | tf_op jit(solution)/shard_map/ppermute | solution.py:38
  21.5 3.9 %collective-permute-start.8 = (bf16[272,512]{1,0:T(8,128)(2,1)S(1)}, bf16[272,512]{1,0:T(8,128)(2,1)S(1)}, u32[]{:S(2)}, u32[]{:S(2)}) collective-permute-start(bf16[272,512]{1,0:T(8,128)(2,1)S(1)} %get-tuple-element.39), channel_id=1, source_target_pairs={{48,0},{50,2},{52,4},{54,6},{56,8},{58,10},{60,12},{62,14},{0,16},... | collective-permute-start | bytes 835592 | tf_op jit(solution)/shard_map/ppermute | solution.py:38
  25.4 3.3 %collective-permute-start.2 = (bf16[128,1024]{1,0:T(8,128)(2,1)S(1)}, bf16[128,1024]{1,0:T(8,128)(2,1)S(1)}, u32[]{:S(2)}, u32[]{:S(2)}) collective-permute-start(bf16[128,1024]{1,0:T(8,128)(2,1)S(1)} %slice.50), channel_id=1, source_target_pairs={{64,0},{66,2},{68,4},{70,6},{72,8},{74,10},{76,12},{78,14},{80,16}... | collective-permute-start | bytes 786440 | tf_op jit(solution)/shard_map/ppermute | solution.py:38
  28.7 4.5 %collective-permute-start.9 = (bf16[136,512]{1,0:T(8,128)(2,1)S(1)}, bf16[136,512]{1,0:T(8,128)(2,1)S(1)}, u32[]{:S(2)}, u32[]{:S(2)}) collective-permute-start(bf16[136,512]{1,0:T(8,128)(2,1)S(1)} %pad_maximum_fusion.3.refs_3_.refs_2_), channel_id=1, source_target_pairs={{32,0},{34,2},{36,4},{38,6},{40,8},{42,10},{44,12},{46,14},{48,16}... | collective-permute-start | bytes 417800 | tf_op jit(solution)/shard_map/ppermute | solution.py:38
  33.2 9.0 %collective-permute-done.9.refs_6_.refs_5_ = bf16[136,512]{1,0:T(8,128)(2,1)S(1)} collective-permute-done((bf16[136,512]{1,0:T(8,128)(2,1)S(1)}, bf16[136,512]{1,0:T(8,128)(2,1)S(1)}, u32[]{:S(2)}, u32[]{:S(2)}) %collective-permute-start.9) | collective-permute-done | bytes 139296 | tf_op jit(solution)/shard_map/ppermute | solution.py:38
  42.2 1.7 %shard_map.104 = (f32[3,2,128,512]{3,2,1,0:T(8,128)S(1)}, f32[4,2,128,128]{3,2,1,0:T(8,128)S(1)}, f32[4,2,128,128]{3,2,1,0:T(8,128)S(1)}) custom-call(bf16[264,1024]{1,0:T(8,128)(2,1)S(1)} %copy-done, bf16[264,1024]{1,0:T(8,128)(2,1)S(1)} %collective-permute-done.refs_1_, bf16[264,1024]{1,0:T(8,128)(2,1)S(1)} %collective-permute-done.1.refs_2_, ...), custom_call_target="tpu_custom_call" | custom-call | tf_op jit(solution)/shard_map/pallas_call | solution.py:261
  43.9 0.7 shard_map.105
  44.6 7.2 %shard_map.106 = (bf16[128,1024]{1,0:T(8,128)(2,1)S(1)}, bf16[128,1024]{1,0:T(8,128)(2,1)S(1)}, bf16[128,1024]{1,0:T(8,128)(2,1)S(1)}, bf16[128,1024]{1,0:T(8,12...) custom-call(bf16[264,1024]{1,0:T(8,128)(2,1)S(1)} %copy-done, ...), custom_call_target="tpu_custom_call" | custom-call | tf_op jit(solution)/shard_map/pallas_call | solution.py:261
  51.8 5.0 %collective-permute-start.16 = (bf16[128,512]{1,0:T(8,128)(2,1)S(1)}, bf16[128,512]{1,0:T(8,128)(2,1)S(1)}, u32[]{:S(2)}, u32[]{:S(2)}) collective-permute-start(bf16[128,512]{1,0:T(8,128)(2,1)S(1)} %get-tuple-element.31), channel_id=1, source_target_pairs={{48,0},{50,2},{52,4},{54,6},{56,8},{58,10},{60,12},{62,14},{0,16},... | collective-permute-start | bytes 393224 | tf_op jit(solution)/shard_map/ppermute | solution.py:38
  56.8 1.6 %collective-permute-start.17 = (bf16[128,512]{1,0:T(8,128)(2,1)S(1)}, bf16[128,512]{1,0:T(8,128)(2,1)S(1)}, u32[]{:S(2)}, u32[]{:S(2)}) collective-permute-start(bf16[128,512]{1,0:T(8,128)(2,1)S(1)} %get-tuple-element.32), channel_id=1, source_target_pairs={{40,0},{42,2},{44,4},{46,6},{48,8},{50,10},{52,12},{54,14},{56,16}... | collective-permute-start | bytes 393224 | tf_op jit(solution)/shard_map/ppermute | solution.py:38
  58.4 2.8 %collective-permute-start.18 = (bf16[128,512]{1,0:T(8,128)(2,1)S(1)}, bf16[128,512]{1,0:T(8,128)(2,1)S(1)}, u32[]{:S(2)}, u32[]{:S(2)}) collective-permute-start(bf16[128,512]{1,0:T(8,128)(2,1)S(1)} %get-tuple-element.33), channel_id=1, source_target_pairs={{16,0},{18,2},{20,4},{22,6},{24,8},{26,10},{28,12},{30,14},{32,16}... | collective-permute-start | bytes 393224 | tf_op jit(solution)/shard_map/ppermute | solution.py:38
  61.3 4.5 %collective-permute-start.13 = (bf16[128,512]{1,0:T(8,128)(2,1)S(1)}, bf16[128,512]{1,0:T(8,128)(2,1)S(1)}, u32[]{:S(2)}, u32[]{:S(2)}) collective-permute-start(bf16[128,512]{1,0:T(8,128)(2,1)S(1)} %get-tuple-element.28), channel_id=1, source_target_pairs={{56,0},{58,2},{60,4},{62,6},{0,8},{2,10},{4,12},{6,14},{8,16},{10,... | collective-permute-start | bytes 393224 | tf_op jit(solution)/shard_map/ppermute | solution.py:38
  65.8 1.3 %collective-permute-done.16 = bf16[128,512]{1,0:T(8,128)(2,1)S(1)} collective-permute-done((bf16[128,512]{1,0:T(8,128)(2,1)S(1)}, bf16[128,512]{1,0:T(8,128)(2,1)S(1)}, u32[]{:S(2)}, u32[]{:S(2)}) %collective-permute-start.16) | collective-permute-done | bytes 131104 | tf_op jit(solution)/shard_map/ppermute | solution.py:38
  67.1 2.5 %collective-permute-start.14 = (bf16[128,512]{1,0:T(8,128)(2,1)S(1)}, bf16[128,512]{1,0:T(8,128)(2,1)S(1)}, u32[]{:S(2)}, u32[]{:S(2)}) collective-permute-start(bf16[128,512]{1,0:T(8,128)(2,1)S(1)} %get-tuple-element.29), channel_id=1, source_target_pairs={{8,0},{10,2},{12,4},{14,6},{16,8},{18,10},{20,12},{22,14},{24,16},... | collective-permute-start | bytes 393224 | tf_op jit(solution)/shard_map/ppermute | solution.py:38
  69.6 2.7 %collective-permute-done.17 = bf16[128,512]{1,0:T(8,128)(2,1)S(1)} collective-permute-done((bf16[128,512]{1,0:T(8,128)(2,1)S(1)}, bf16[128,512]{1,0:T(8,128)(2,1)S(1)}, u32[]{:S(2)}, u32[]{:S(2)}) %collective-permute-start.17) | collective-permute-done | bytes 131104 | tf_op jit(solution)/shard_map/ppermute | solution.py:38
  72.4 3.6 %collective-permute-done.19 = bf16[128,512]{1,0:T(8,128)(2,1)S(1)} collective-permute-done((bf16[128,512]{1,0:T(8,128)(2,1)S(1)}, bf16[128,512]{1,0:T(8,128)(2,1)S(1)}, u32[]{:S(2)}, u32[]{:S(2)}) %collective-permute-start.19) | collective-permute-done | bytes 131104 | tf_op jit(solution)/shard_map/ppermute | solution.py:38
  75.9 2.4 %collective-permute-done.14 = bf16[128,512]{1,0:T(8,128)(2,1)S(1)} collective-permute-done((bf16[128,512]{1,0:T(8,128)(2,1)S(1)}, bf16[128,512]{1,0:T(8,128)(2,1)S(1)}, u32[]{:S(2)}, u32[]{:S(2)}) %collective-permute-start.14) | collective-permute-done | bytes 131104 | tf_op jit(solution)/shard_map/ppermute | solution.py:38
  78.3 3.0 %collective-permute-done.15 = bf16[128,512]{1,0:T(8,128)(2,1)S(1)} collective-permute-done((bf16[128,512]{1,0:T(8,128)(2,1)S(1)}, bf16[128,512]{1,0:T(8,128)(2,1)S(1)}, u32[]{:S(2)}, u32[]{:S(2)}) %collective-permute-start.15) | collective-permute-done | bytes 131104 | tf_op jit(solution)/shard_map/ppermute | solution.py:38
  81.5 3.1 %collective-permute-start.20 = (bf16[64,512]{1,0:T(8,128)(2,1)S(1)}, bf16[64,512]{1,0:T(8,128)(2,1)S(1)}, u32[]{:S(2)}, u32[]{:S(2)}) collective-permute-start(bf16[64,512]{1,0:T(8,128)(2,1)S(1)} %broadcast_select_fusion.2), channel_id=1, source_target_pairs={{0,1},{1,0},{2,3},{3,2},{4,5},{5,4},{6,7},{7,6},{8,9},{9,8},{10,11... | collective-permute-start | bytes 196616 | tf_op jit(solution)/shard_map/ppermute | solution.py:42
  84.6 3.5 %collective-permute-start.10 = (bf16[128,1024]{1,0:T(8,128)(2,1)S(1)}, bf16[128,1024]{1,0:T(8,128)(2,1)S(1)}, u32[]{:S(2)}, u32[]{:S(2)}) collective-permute-start(bf16[128,1024]{1,0:T(8,128)(2,1)S(1)} %get-tuple-element.24), channel_id=1, source_target_pairs={{192,0},{194,2},{196,4},{198,6},{200,8},{202,10},{204,12},{206,14}... | collective-permute-start | bytes 786440 | tf_op jit(solution)/shard_map/ppermute | solution.py:38
  88.1 5.9 %collective-permute-start.11 = (bf16[128,1024]{1,0:T(8,128)(2,1)S(1)}, bf16[128,1024]{1,0:T(8,128)(2,1)S(1)}, u32[]{:S(2)}, u32[]{:S(2)}) collective-permute-start(bf16[128,1024]{1,0:T(8,128)(2,1)S(1)} %get-tuple-element.25), channel_id=1, source_target_pairs={{64,0},{66,2},{68,4},{70,6},{72,8},{74,10},{76,12},{78,14},{80,16}... | collective-permute-start | bytes 786440 | tf_op jit(solution)/shard_map/ppermute | solution.py:38
  94.0 1.5 %collective-permute-start.12 = (bf16[128,1024]{1,0:T(8,128)(2,1)S(1)}, bf16[128,1024]{1,0:T(8,128)(2,1)S(1)}, u32[]{:S(2)}, u32[]{:S(2)}) collective-permute-start(bf16[128,1024]{1,0:T(8,128)(2,1)S(1)} %get-tuple-element.26), channel_id=1, source_target_pairs={{128,0},{130,2},{132,4},{134,6},{136,8},{138,10},{140,12},{142,14}... | collective-permute-start | bytes 786440 | tf_op jit(solution)/shard_map/ppermute | solution.py:38
  96.8 3.5 %collective-permute-done.10 = bf16[128,1024]{1,0:T(8,128)(2,1)S(1)} collective-permute-done((bf16[128,1024]{1,0:T(8,128)(2,1)S(1)}, bf16[128,1024]{1,0:T(8,128)(2,1)S(1)}, u32[]{:S(2)}, u32[]{:S(2)}) %collective-permute-start.10) | collective-permute-done | bytes 262176 | tf_op jit(solution)/shard_map/ppermute | solution.py:38
  100.3 4.7 %collective-permute-done.11 = bf16[128,1024]{1,0:T(8,128)(2,1)S(1)} collective-permute-done((bf16[128,1024]{1,0:T(8,128)(2,1)S(1)}, bf16[128,1024]{1,0:T(8,128)(2,1)S(1)}, u32[]{:S(2)}, u32[]{:S(2)}) %collective-permute-start.11) | collective-permute-done | bytes 262176 | tf_op jit(solution)/shard_map/ppermute | solution.py:38
  104.9 1.9 %collective-permute-done.12 = bf16[128,1024]{1,0:T(8,128)(2,1)S(1)} collective-permute-done((bf16[128,1024]{1,0:T(8,128)(2,1)S(1)}, bf16[128,1024]{1,0:T(8,128)(2,1)S(1)}, u32[]{:S(2)}, u32[]{:S(2)}) %collective-permute-start.12) | collective-permute-done | bytes 262176 | tf_op jit(solution)/shard_map/ppermute | solution.py:38
  106.8 0.9 add_convert_fusion
  (37 shorter events, 2.3 us)
Async XLA Ops:
  0.6 9.2 %copy-start.1 = (s32[128]{0:T(128)S(1)}, s32[128]{0:T(128)}, u32[]{:S(2)}) copy-start(s32[128]{0:T(128)} %param.14) | copy-start | bytes 1540
  2.8 22.6 %collective-permute-start = (bf16[264,1024]{1,0:T(8,128)(2,1)}, bf16[264,1024]{1,0:T(8,128)(2,1)S(1)}, u32[]{:S(2)}, u32[]{:S(2)}) collective-permute-start(bf16[264,1024]{1,0:T(8,128)(2,1)} %shard_map.103.refs_0_), channel_id=1, source_target_pairs={{64,0},{66,2},{68,4},{70,6},{72,8},{74,10},{76,12},{78,14},{80,16}... | collective-permute-start | bytes 1622024 | tf_op jit(solution)/shard_map/ppermute | solution.py:38
  5.8 15.2 %collective-permute-start.1 = (bf16[264,1024]{1,0:T(8,128)(2,1)}, bf16[264,1024]{1,0:T(8,128)(2,1)S(1)}, u32[]{:S(2)}, u32[]{:S(2)}) collective-permute-start(bf16[264,1024]{1,0:T(8,128)(2,1)} %shard_map.103.refs_0_), channel_id=1, source_target_pairs={{192,0},{194,2},{196,4},{198,6},{200,8},{202,10},{204,12},{206,14}... | collective-permute-start | bytes 1622024 | tf_op jit(solution)/shard_map/ppermute | solution.py:38
  5.8 36.3 %copy-start = (bf16[264,1024]{1,0:T(8,128)(2,1)S(1)}, bf16[264,1024]{1,0:T(8,128)(2,1)}, u32[]{:S(2)}) copy-start(bf16[264,1024]{1,0:T(8,128)(2,1)} %shard_map.103.refs_0_) | copy-start | bytes 1622020
  6.8 5.9 %collective-permute-start.4 = (bf16[64,512]{1,0:T(8,128)(2,1)S(1)}, bf16[64,512]{1,0:T(8,128)(2,1)S(1)}, u32[]{:S(2)}, u32[]{:S(2)}) collective-permute-start(bf16[64,512]{1,0:T(8,128)(2,1)S(1)} %broadcast_select_fusion.6), channel_id=1, source_target_pairs={{0,1},{1,0},{2,3},{3,2},{4,5},{5,4},{6,7},{7,6},{8,9},{9,8},{10,11... | collective-permute-start | bytes 196616 | tf_op jit(solution)/shard_map/ppermute | solution.py:42
  12.7 8.4 %collective-permute-start.5 = (bf16[136,512]{1,0:T(8,128)(2,1)S(1)}, bf16[136,512]{1,0:T(8,128)(2,1)S(1)}, u32[]{:S(2)}, u32[]{:S(2)}) collective-permute-start(bf16[136,512]{1,0:T(8,128)(2,1)S(1)} %pad_maximum_fusion.3.refs_3_.refs_2_), channel_id=1, source_target_pairs={{8,0},{10,2},{12,4},{14,6},{16,8},{18,10},{20,12},{22,14},{24,16},... | collective-permute-start | bytes 417800 | tf_op jit(solution)/shard_map/ppermute | solution.py:38
  12.9 8.3 %collective-permute-start.7 = (bf16[136,512]{1,0:T(8,128)(2,1)S(1)}, bf16[136,512]{1,0:T(8,128)(2,1)S(1)}, u32[]{:S(2)}, u32[]{:S(2)}) collective-permute-start(bf16[136,512]{1,0:T(8,128)(2,1)S(1)} %pad_maximum_fusion.3.refs_3_.refs_2_), channel_id=1, source_target_pairs={{56,0},{58,2},{60,4},{62,6},{0,8},{2,10},{4,12},{6,14},{8,16},{10,... | collective-permute-start | bytes 417800 | tf_op jit(solution)/shard_map/ppermute | solution.py:38
  21.0 22.9 %collective-permute-start.3 = (bf16[136,1024]{1,0:T(8,128)(2,1)S(1)}, bf16[136,1024]{1,0:T(8,128)(2,1)S(1)}, u32[]{:S(2)}, u32[]{:S(2)}) collective-permute-start(bf16[136,1024]{1,0:T(8,128)(2,1)S(1)} %slice.51), channel_id=1, source_target_pairs={{192,0},{194,2},{196,4},{198,6},{200,8},{202,10},{204,12},{206,14}... | collective-permute-start | bytes 835592 | tf_op jit(solution)/shard_map/ppermute | solution.py:38
  21.2 23.4 %collective-permute-start.6 = (bf16[272,512]{1,0:T(8,128)(2,1)S(1)}, bf16[272,512]{1,0:T(8,128)(2,1)S(1)}, u32[]{:S(2)}, u32[]{:S(2)}) collective-permute-start(bf16[272,512]{1,0:T(8,128)(2,1)S(1)} %get-tuple-element.40), channel_id=1, source_target_pairs={{16,0},{18,2},{20,4},{22,6},{24,8},{26,10},{28,12},{30,14},{32,16}... | collective-permute-start | bytes 835592 | tf_op jit(solution)/shard_map/ppermute | solution.py:38
  21.5 23.0 %collective-permute-start.8 = (bf16[272,512]{1,0:T(8,128)(2,1)S(1)}, bf16[272,512]{1,0:T(8,128)(2,1)S(1)}, u32[]{:S(2)}, u32[]{:S(2)}) collective-permute-start(bf16[272,512]{1,0:T(8,128)(2,1)S(1)} %get-tuple-element.39), channel_id=1, source_target_pairs={{48,0},{50,2},{52,4},{54,6},{56,8},{58,10},{60,12},{62,14},{0,16},... | collective-permute-start | bytes 835592 | tf_op jit(solution)/shard_map/ppermute | solution.py:38
  25.4 18.4 %collective-permute-start.2 = (bf16[128,1024]{1,0:T(8,128)(2,1)S(1)}, bf16[128,1024]{1,0:T(8,128)(2,1)S(1)}, u32[]{:S(2)}, u32[]{:S(2)}) collective-permute-start(bf16[128,1024]{1,0:T(8,128)(2,1)S(1)} %slice.50), channel_id=1, source_target_pairs={{64,0},{66,2},{68,4},{70,6},{72,8},{74,10},{76,12},{78,14},{80,16}... | collective-permute-start | bytes 786440 | tf_op jit(solution)/shard_map/ppermute | solution.py:38
  28.7 13.5 %collective-permute-start.9 = (bf16[136,512]{1,0:T(8,128)(2,1)S(1)}, bf16[136,512]{1,0:T(8,128)(2,1)S(1)}, u32[]{:S(2)}, u32[]{:S(2)}) collective-permute-start(bf16[136,512]{1,0:T(8,128)(2,1)S(1)} %pad_maximum_fusion.3.refs_3_.refs_2_), channel_id=1, source_target_pairs={{32,0},{34,2},{36,4},{38,6},{40,8},{42,10},{44,12},{46,14},{48,16}... | collective-permute-start | bytes 417800 | tf_op jit(solution)/shard_map/ppermute | solution.py:38
  51.8 15.3 %collective-permute-start.16 = (bf16[128,512]{1,0:T(8,128)(2,1)S(1)}, bf16[128,512]{1,0:T(8,128)(2,1)S(1)}, u32[]{:S(2)}, u32[]{:S(2)}) collective-permute-start(bf16[128,512]{1,0:T(8,128)(2,1)S(1)} %get-tuple-element.31), channel_id=1, source_target_pairs={{48,0},{50,2},{52,4},{54,6},{56,8},{58,10},{60,12},{62,14},{0,16},... | collective-permute-start | bytes 393224 | tf_op jit(solution)/shard_map/ppermute | solution.py:38
  56.8 15.5 %collective-permute-start.17 = (bf16[128,512]{1,0:T(8,128)(2,1)S(1)}, bf16[128,512]{1,0:T(8,128)(2,1)S(1)}, u32[]{:S(2)}, u32[]{:S(2)}) collective-permute-start(bf16[128,512]{1,0:T(8,128)(2,1)S(1)} %get-tuple-element.32), channel_id=1, source_target_pairs={{40,0},{42,2},{44,4},{46,6},{48,8},{50,10},{52,12},{54,14},{56,16}... | collective-permute-start | bytes 393224 | tf_op jit(solution)/shard_map/ppermute | solution.py:38
  58.4 13.9 %collective-permute-start.18 = (bf16[128,512]{1,0:T(8,128)(2,1)S(1)}, bf16[128,512]{1,0:T(8,128)(2,1)S(1)}, u32[]{:S(2)}, u32[]{:S(2)}) collective-permute-start(bf16[128,512]{1,0:T(8,128)(2,1)S(1)} %get-tuple-element.33), channel_id=1, source_target_pairs={{16,0},{18,2},{20,4},{22,6},{24,8},{26,10},{28,12},{30,14},{32,16}... | collective-permute-start | bytes 393224 | tf_op jit(solution)/shard_map/ppermute | solution.py:38
  61.3 14.7 %collective-permute-start.19 = (bf16[128,512]{1,0:T(8,128)(2,1)S(1)}, bf16[128,512]{1,0:T(8,128)(2,1)S(1)}, u32[]{:S(2)}, u32[]{:S(2)}) collective-permute-start(bf16[128,512]{1,0:T(8,128)(2,1)S(1)} %get-tuple-element.34), channel_id=1, source_target_pairs={{24,0},{26,2},{28,4},{30,6},{32,8},{34,10},{36,12},{38,14},{40,16}... | collective-permute-start | bytes 393224 | tf_op jit(solution)/shard_map/ppermute | solution.py:38
  61.3 14.7 %collective-permute-start.13 = (bf16[128,512]{1,0:T(8,128)(2,1)S(1)}, bf16[128,512]{1,0:T(8,128)(2,1)S(1)}, u32[]{:S(2)}, u32[]{:S(2)}) collective-permute-start(bf16[128,512]{1,0:T(8,128)(2,1)S(1)} %get-tuple-element.28), channel_id=1, source_target_pairs={{56,0},{58,2},{60,4},{62,6},{0,8},{2,10},{4,12},{6,14},{8,16},{10,... | collective-permute-start | bytes 393224 | tf_op jit(solution)/shard_map/ppermute | solution.py:38
  67.1 11.2 %collective-permute-start.14 = (bf16[128,512]{1,0:T(8,128)(2,1)S(1)}, bf16[128,512]{1,0:T(8,128)(2,1)S(1)}, u32[]{:S(2)}, u32[]{:S(2)}) collective-permute-start(bf16[128,512]{1,0:T(8,128)(2,1)S(1)} %get-tuple-element.29), channel_id=1, source_target_pairs={{8,0},{10,2},{12,4},{14,6},{16,8},{18,10},{20,12},{22,14},{24,16},... | collective-permute-start | bytes 393224 | tf_op jit(solution)/shard_map/ppermute | solution.py:38
  72.3 9.0 %collective-permute-start.15 = (bf16[128,512]{1,0:T(8,128)(2,1)S(1)}, bf16[128,512]{1,0:T(8,128)(2,1)S(1)}, u32[]{:S(2)}, u32[]{:S(2)}) collective-permute-start(bf16[128,512]{1,0:T(8,128)(2,1)S(1)} %get-tuple-element.30), channel_id=1, source_target_pairs={{32,0},{34,2},{36,4},{38,6},{40,8},{42,10},{44,12},{46,14},{48,16}... | collective-permute-start | bytes 393224 | tf_op jit(solution)/shard_map/ppermute | solution.py:38
  81.5 14.0 %collective-permute-start.20 = (bf16[64,512]{1,0:T(8,128)(2,1)S(1)}, bf16[64,512]{1,0:T(8,128)(2,1)S(1)}, u32[]{:S(2)}, u32[]{:S(2)}) collective-permute-start(bf16[64,512]{1,0:T(8,128)(2,1)S(1)} %broadcast_select_fusion.2), channel_id=1, source_target_pairs={{0,1},{1,0},{2,3},{3,2},{4,5},{5,4},{6,7},{7,6},{8,9},{9,8},{10,11... | collective-permute-start | bytes 196616 | tf_op jit(solution)/shard_map/ppermute | solution.py:42
  84.6 15.7 %collective-permute-start.10 = (bf16[128,1024]{1,0:T(8,128)(2,1)S(1)}, bf16[128,1024]{1,0:T(8,128)(2,1)S(1)}, u32[]{:S(2)}, u32[]{:S(2)}) collective-permute-start(bf16[128,1024]{1,0:T(8,128)(2,1)S(1)} %get-tuple-element.24), channel_id=1, source_target_pairs={{192,0},{194,2},{196,4},{198,6},{200,8},{202,10},{204,12},{206,14}... | collective-permute-start | bytes 786440 | tf_op jit(solution)/shard_map/ppermute | solution.py:38
  88.1 16.8 %collective-permute-start.11 = (bf16[128,1024]{1,0:T(8,128)(2,1)S(1)}, bf16[128,1024]{1,0:T(8,128)(2,1)S(1)}, u32[]{:S(2)}, u32[]{:S(2)}) collective-permute-start(bf16[128,1024]{1,0:T(8,128)(2,1)S(1)} %get-tuple-element.25), channel_id=1, source_target_pairs={{64,0},{66,2},{68,4},{70,6},{72,8},{74,10},{76,12},{78,14},{80,16}... | collective-permute-start | bytes 786440 | tf_op jit(solution)/shard_map/ppermute | solution.py:38
  94.0 12.8 %collective-permute-start.12 = (bf16[128,1024]{1,0:T(8,128)(2,1)S(1)}, bf16[128,1024]{1,0:T(8,128)(2,1)S(1)}, u32[]{:S(2)}, u32[]{:S(2)}) collective-permute-start(bf16[128,1024]{1,0:T(8,128)(2,1)S(1)} %get-tuple-element.26), channel_id=1, source_target_pairs={{128,0},{130,2},{132,4},{134,6},{136,8},{138,10},{140,12},{142,14}... | collective-permute-start | bytes 786440 | tf_op jit(solution)/shard_map/ppermute | solution.py:38

commit v3 on v2

--- a/solution.py
+++ b/solution.py
@@ -15,6 +15,7 @@
 GRID_Z = 8
 ROW_SHIFTS = (0, 1, -1, 2)
 AUX = 8
+SPLIT = 1
 LOG2E = math.log2(math.e)
 SCALE = HEAD_DIM ** (-0.5)
 
@@ -94,7 +95,7 @@
     qs, gs, lse_s, dot_s, first_s, last_s, ks, vs, kts = take(9)
     dqt = take(1)[0] if dq_final else dq_refs[0]
     dk, dv = take(2) if kv_final else dkv_refs
-    starts, listed, counts = take(3)
+    starts, listed, counts, limits = take(4)
     rows = 128
     heads = row_refs[0].shape[1] // HEAD_DIM
     kv_heads = col_refs[0].shape[1] // HEAD_DIM // 2
@@ -142,6 +143,8 @@
             some = (col_starts[c] <= most) & (col_starts[c] + (rows - 1) >= least)
             count = count + some.astype(jnp.int32)
         counts[r] = count
+        limits[0, r] = jnp.min(last)
+        limits[1, r] = jnp.max(first)
     filled = 0
     for old in dq_in:
         dqt[filled : filled + old.shape[0]] = old[...]
@@ -155,41 +158,49 @@
         dk[...] = jnp.zeros_like(dk)
         dv[...] = jnp.zeros_like(dv)
 
-    def pair(r, one, two, start_one, start_two):
-        along = lax.broadcasted_iota(jnp.int32, (rows, wide), 0)
-        last = last_s[r]
-        first = first_s[r]
-        visible = [
-            (along + start <= last) & (along + start >= first) for start in (start_one, start_two)
-        ]
+    def pair(r, one, two, start_one, start_two, masked):
+        part_wide = wide // SPLIT
+        heads_starts = (start_one, start_two)
+        if masked:
+            along = lax.broadcasted_iota(jnp.int32, (rows, part_wide), 0)
+            last = last_s[r, :, 0:part_wide]
+            first = first_s[r, :, 0:part_wide]
+            visible = [(along + start <= last) & (along + start >= first) for start in heads_starts]
         for j in range(kv_heads):
-            span = slice(j * wide, (j + 1) * wide)
-            q = qs[r, span, :]
-            g = gs[r, span, :]
             keys = jnp.concatenate([ks[one, j], ks[two, j]], axis=0)
             values = jnp.concatenate([vs[one, j], vs[two, j]], axis=0)
             keys_turned = jnp.concatenate([kts[one, j], kts[two, j]], axis=1)
-            scores = dot(keys, q, NT)
-            prob_grad = dot(values, g, NT)
-            lse = lse_s[r, :, span]
-            out_dot = dot_s[r, :, span]
-            probs_both = []
-            grads_both = []
-            for at in range(2):
-                part = slice(at * rows, (at + 1) * rows)
-                probs = jnp.exp2(scores[part] * (SCALE * LOG2E) - lse)
-                probs = jnp.where(visible[at], probs, 0.0)
-                grads_both.append((probs * (prob_grad[part] - out_dot) * SCALE).astype(jnp.bfloat16))
-                probs_both.append(probs.astype(jnp.bfloat16))
-            probs = jnp.concatenate(probs_both, axis=0)
-            score_grad = jnp.concatenate(grads_both, axis=0)
-            value_update = dot(probs, g, NN)
-            key_update = dot(score_grad, q, NN)
+            value_update = None
+            for piece in range(SPLIT):
+                low = j * wide + piece * part_wide
+                span = slice(low, low + part_wide)
+                q = qs[r, span, :]
+                g = gs[r, span, :]
+                scores = dot(keys, q, NT)
+                prob_grad = dot(values, g, NT)
+                lse = lse_s[r, :, span]
+                out_dot = dot_s[r, :, span]
+                probs_both = []
+                grads_both = []
+                for at in range(2):
+                    part = slice(at * rows, (at + 1) * rows)
+                    probs = jnp.exp2(scores[part] * (SCALE * LOG2E) - lse)
+                    if masked:
+                        probs = jnp.where(visible[at], probs, 0.0)
+                    grads_both.append((probs * (prob_grad[part] - out_dot) * SCALE).astype(jnp.bfloat16))
+                    probs_both.append(probs.astype(jnp.bfloat16))
+                probs = jnp.concatenate(probs_both, axis=0)
+                score_grad = jnp.concatenate(grads_both, axis=0)
+                piece_value = dot(probs, g, NN)
+                piece_key = dot(score_grad, q, NN)
+                value_update = piece_value if value_update is None else value_update + piece_value
+                key_update = piece_key if piece == 0 else key_update + piece_key
+                here = slice(piece * part_wide, (piece + 1) * part_wide)
+                dqt[r, j, :, here] += dot(keys_turned, score_grad, NN)
             dv[one, j] += value_update[:rows]
             dv[two, j] += value_update[rows:]
             dk[one, j] += key_update[:rows]
             dk[two, j] += key_update[rows:]
-            dqt[r, j] += dot(keys_turned, score_grad, NN)
 
     def row_block(r, carry):
         count = counts[r]
@@ -198,7 +209,12 @@
             one = listed[r, 2 * at]
             both = 2 * at + 1 < count
             two = jnp.where(both, listed[r, 2 * at + 1], one)
-            pair(r, one, two, starts[one], jnp.where(both, starts[two], 1 << 20))
+            start_one = starts[one]
+            start_two = jnp.where(both, starts[two], 1 << 20)
+            top = jnp.maximum(start_one, start_two) + (rows - 1)
+            whole = (top <= limits[0, r]) & (jnp.minimum(start_one, start_two) >= limits[1, r])
+            pl.when(whole)(lambda: pair(r, one, two, start_one, start_two, False))
+            pl.when(jnp.logical_not(whole))(lambda: pair(r, one, two, start_one, start_two, True))
             return inner
 
         return lax.fori_loop(0, (count + 1) // 2, trip, carry)
@@ -254,6 +270,7 @@
         pltpu.SMEM((n_cols,), jnp.int32),
         pltpu.SMEM((n_rows, n_cols + 1), jnp.int32),
         pltpu.SMEM((n_rows,), jnp.int32),
+        pltpu.SMEM((2, n_rows), jnp.int32),
     ]
     body = functools.partial(
         grads_kernel, row_places, col_places, len(dq_in), bool(kv_in), dq_final, kv_final
@@ -330,10 +347,21 @@
     two_place = ((0, 0), (1, 0), (1, rows))
     last_place = ((3, 0), (4, 0), (4, rows))
 
-    dq_first, kv_near = call_grads(first_rows, first_places, near, near_places, (), (), False, False)
-    dq_two, near_parts = call_grads(two_rows, (two_place,), near, near_places, (), kv_near, False, True)
+    dq_first, kv_near = call_grads(
+        first_rows, first_places, near, near_places, (), (), False, False
+    )
+    dq_two, near_parts = call_grads(
+        two_rows, (two_place,), near, near_places, (), kv_near, False, True
+    )
     dq_parts, far_parts = call_grads(
-        first_rows + two_rows, first_places + (last_place,), far, far_places, (*dq_first, *dq_two), (), True, True
+        first_rows + two_rows,
+        first_places + (last_place,),
+        far,
+        far_places,
+        (*dq_first, *dq_two),
+        (),
+        True,
+        True,
     )
 
     parts = dict(zip(near_shifts + far_shifts, (*near_parts, *far_parts)))

time: 108 us -> 107 us (level)
  the two profiles are of different devices: /device:TPU:96 before, /device:TPU:34 now
where the time goes in v3:
time: 107 us; the launch traced here: 106 us
  waiting for transfers between devices  53.9 us (50%)
  starting transfers between devices  35.4 us (33%)
  Pallas kernels  12.8 us (12%)
  other arithmetic  2.44 us (2%)
    ppermute x19, waiting for transfers between devices, shifted(): return lax.ppermute(value, 'ctx', pairs)  49.9 us
    ppermute x19, starting transfers between devices, shifted(): return lax.ppermute(value, 'ctx', pairs)  31 us
    pallas_call x3, Pallas kernels, call_grads(): pl.pallas_call(body, out_shape=out_shape, in_specs=[VMEM_SPEC] * len(oper...  10.7 us
    ppermute x2, starting transfers between devices, swap_head(): return lax.ppermute(value, 'head', [(0, 1), (1, 0)])  4.42 us
    ppermute x2, waiting for transfers between devices, swap_head(): return lax.ppermute(value, 'head', [(0, 1), (1, 0)])  4.03 us
    pallas_call x1, Pallas kernels, shards(): pl.pallas_call(pack_rows_kernel, out_shape=shape((2 * rows + AUX, width),...  2.18 us
  transfers between devices with their start and end apart: 21, of which 10 were waited for; matrix products, arithmetic and copies ran while one was open for 2% of the time, Pallas kernels for 6%

profile of v3, /device:TPU:34, one launch (start us, length us, event | category | flops | bytes accessed | tf_op | source)
XLA Modules:
  0.0 106.4 jit_solution(7954093583683518001)
XLA Ops:
  0.6 2.2 %shard_map.103.refs_0_ = bf16[264,1024]{1,0:T(8,128)(2,1)} custom-call(bf16[128,1024]{1,0:T(8,128)(2,1)} %q_ref.1, bf16[128,1024]{1,0:T(8,128)(2,1)} %o_ref.1, bf16[128,1024]{1,0:T(8,128)(2,1)} %g_ref.1, f32[8,128]{1,0:T(8,128)} %lse_ref.1, s32[1,128]{1,0:T(1,128)} %bitcast.3, s32[1,128]{1,0:T(1,128)} %bitcast.2), custom_call_target="tpu_custom_call" | custom-call | tf_op jit(solution)/shard_map/pallas_call | solution.py:302
  2.8 3.0 %collective-permute-start = (bf16[264,1024]{1,0:T(8,128)(2,1)}, bf16[264,1024]{1,0:T(8,128)(2,1)S(1)}, u32[]{:S(2)}, u32[]{:S(2)}) collective-permute-start(bf16[264,1024]{1,0:T(8,128)(2,1)} %shard_map.103.refs_0_), channel_id=1, source_target_pairs={{64,0},{66,2},{68,4},{70,6},{72,8},{74,10},{76,12},{78,14},{80,16}... | collective-permute-start | bytes 1622024 | tf_op jit(solution)/shard_map/ppermute | solution.py:39
  5.8 0.9 fusion.2
  6.8 2.2 %collective-permute-start.4 = (bf16[64,512]{1,0:T(8,128)(2,1)S(1)}, bf16[64,512]{1,0:T(8,128)(2,1)S(1)}, u32[]{:S(2)}, u32[]{:S(2)}) collective-permute-start(bf16[64,512]{1,0:T(8,128)(2,1)S(1)} %broadcast_select_fusion.6), channel_id=1, source_target_pairs={{0,1},{1,0},{2,3},{3,2},{4,5},{5,4},{6,7},{7,6},{8,9},{9,8},{10,11... | collective-permute-start | bytes 196616 | tf_op jit(solution)/shard_map/ppermute | solution.py:43
  9.0 3.6 %collective-permute-done.4 = bf16[64,512]{1,0:T(8,128)(2,1)S(1)} collective-permute-done((bf16[64,512]{1,0:T(8,128)(2,1)S(1)}, bf16[64,512]{1,0:T(8,128)(2,1)S(1)}, u32[]{:S(2)}, u32[]{:S(2)}) %collective-permute-start.4) | collective-permute-done | bytes 65568 | tf_op jit(solution)/shard_map/ppermute | solution.py:43
  12.7 0.2 collective-permute-start.5
  12.9 1.9 %collective-permute-start.7 = (bf16[136,512]{1,0:T(8,128)(2,1)S(1)}, bf16[136,512]{1,0:T(8,128)(2,1)S(1)}, u32[]{:S(2)}, u32[]{:S(2)}) collective-permute-start(bf16[136,512]{1,0:T(8,128)(2,1)S(1)} %pad_maximum_fusion.3.refs_3_.refs_2_), channel_id=1, source_target_pairs={{56,0},{58,2},{60,4},{62,6},{0,8},{2,10},{4,12},{6,14},{8,16},{10,... | collective-permute-start | bytes 417800 | tf_op jit(solution)/shard_map/ppermute | solution.py:39
  14.8 6.2 %collective-permute-done.1.refs_2_ = bf16[264,1024]{1,0:T(8,128)(2,1)S(1)} collective-permute-done((bf16[264,1024]{1,0:T(8,128)(2,1)}, bf16[264,1024]{1,0:T(8,128)(2,1)S(1)}, u32[]{:S(2)}, u32[]{:S(2)}) %collective-permute-start.1) | collective-permute-done | bytes 540704 | tf_op jit(solution)/shard_map/ppermute | solution.py:39
  21.1 0.6 collective-permute-done.7.refs_5_.refs_4_
  21.8 4.9 %collective-permute-start.6 = (bf16[272,512]{1,0:T(8,128)(2,1)S(1)}, bf16[272,512]{1,0:T(8,128)(2,1)S(1)}, u32[]{:S(2)}, u32[]{:S(2)}) collective-permute-start(bf16[272,512]{1,0:T(8,128)(2,1)S(1)} %get-tuple-element.40), channel_id=1, source_target_pairs={{16,0},{18,2},{20,4},{22,6},{24,8},{26,10},{28,12},{30,14},{32,16}... | collective-permute-start | bytes 835592 | tf_op jit(solution)/shard_map/ppermute | solution.py:39
  26.7 3.3 %collective-permute-start.2 = (bf16[128,1024]{1,0:T(8,128)(2,1)S(1)}, bf16[128,1024]{1,0:T(8,128)(2,1)S(1)}, u32[]{:S(2)}, u32[]{:S(2)}) collective-permute-start(bf16[128,1024]{1,0:T(8,128)(2,1)S(1)} %slice.50), channel_id=1, source_target_pairs={{64,0},{66,2},{68,4},{70,6},{72,8},{74,10},{76,12},{78,14},{80,16}... | collective-permute-start | bytes 786440 | tf_op jit(solution)/shard_map/ppermute | solution.py:39
  30.0 3.8 %collective-permute-start.9 = (bf16[136,512]{1,0:T(8,128)(2,1)S(1)}, bf16[136,512]{1,0:T(8,128)(2,1)S(1)}, u32[]{:S(2)}, u32[]{:S(2)}) collective-permute-start(bf16[136,512]{1,0:T(8,128)(2,1)S(1)} %pad_maximum_fusion.3.refs_3_.refs_2_), channel_id=1, source_target_pairs={{32,0},{34,2},{36,4},{38,6},{40,8},{42,10},{44,12},{46,14},{48,16}... | collective-permute-start | bytes 417800 | tf_op jit(solution)/shard_map/ppermute | solution.py:39
  33.8 11.5 %collective-permute-done.9.refs_6_.refs_5_ = bf16[136,512]{1,0:T(8,128)(2,1)S(1)} collective-permute-done((bf16[136,512]{1,0:T(8,128)(2,1)S(1)}, bf16[136,512]{1,0:T(8,128)(2,1)S(1)}, u32[]{:S(2)}, u32[]{:S(2)}) %collective-permute-start.9) | collective-permute-done | bytes 139296 | tf_op jit(solution)/shard_map/ppermute | solution.py:39
  45.3 4.5 %shard_map.104 = (f32[3,2,128,512]{3,2,1,0:T(8,128)S(1)}, f32[4,2,128,128]{3,2,1,0:T(8,128)S(1)}, f32[4,2,128,128]{3,2,1,0:T(8,128)S(1)}) custom-call(bf16[264,1024]{1,0:T(8,128)(2,1)S(1)} %copy-done, bf16[264,1024]{1,0:T(8,128)(2,1)S(1)} %collective-permute-done.refs_1_, bf16[264,1024]{1,0:T(8,128)(2,1)S(1)} %collective-permute-done.1.refs_2_, ...), custom_call_target="tpu_custom_call" | custom-call | tf_op jit(solution)/shard_map/pallas_call | solution.py:278
  49.9 1.7 %shard_map.105 = (f32[1,2,128,512]{3,2,1,0:T(8,128)S(1)}, bf16[128,512]{1,0:T(8,128)(2,1)S(1)}, bf16[128,512]{1,0:T(8,128)(2,1)S(1)}, bf16[128,512]{1,0:T(8,128)(2,1)S(1)}, bf16[128,512]{1,0:T(8,128)(2,1)S(1)}) custom-call(bf16[128,1024]{1,0:T(8,128)(2,1)S(1)} %collective-permute-done.2.refs_0_.refs_3_, ...), custom_call_target="tpu_custom_call" | custom-call | tf_op jit(solution)/shard_map/pallas_call | solution.py:278
  51.6 4.4 %shard_map.106 = (bf16[128,1024]{1,0:T(8,128)(2,1)S(1)}, bf16[128,1024]{1,0:T(8,128)(2,1)S(1)}, bf16[128,1024]{1,0:T(8,128)(2,1)S(1)}, bf16[128,1024]{1,0:T(8,12...) custom-call(bf16[264,1024]{1,0:T(8,128)(2,1)S(1)} %copy-done, ...), custom_call_target="tpu_custom_call" | custom-call | tf_op jit(solution)/shard_map/pallas_call | solution.py:278
  56.1 4.5 %collective-permute-start.17 = (bf16[128,512]{1,0:T(8,128)(2,1)S(1)}, bf16[128,512]{1,0:T(8,128)(2,1)S(1)}, u32[]{:S(2)}, u32[]{:S(2)}) collective-permute-start(bf16[128,512]{1,0:T(8,128)(2,1)S(1)} %get-tuple-element.32), channel_id=1, source_target_pairs={{40,0},{42,2},{44,4},{46,6},{48,8},{50,10},{52,12},{54,14},{56,16}... | collective-permute-start | bytes 393224 | tf_op jit(solution)/shard_map/ppermute | solution.py:39
  60.6 1.8 %collective-permute-start.18 = (bf16[128,512]{1,0:T(8,128)(2,1)S(1)}, bf16[128,512]{1,0:T(8,128)(2,1)S(1)}, u32[]{:S(2)}, u32[]{:S(2)}) collective-permute-start(bf16[128,512]{1,0:T(8,128)(2,1)S(1)} %get-tuple-element.33), channel_id=1, source_target_pairs={{16,0},{18,2},{20,4},{22,6},{24,8},{26,10},{28,12},{30,14},{32,16}... | collective-permute-start | bytes 393224 | tf_op jit(solution)/shard_map/ppermute | solution.py:39
  62.4 1.7 %collective-permute-start.19 = (bf16[128,512]{1,0:T(8,128)(2,1)S(1)}, bf16[128,512]{1,0:T(8,128)(2,1)S(1)}, u32[]{:S(2)}, u32[]{:S(2)}) collective-permute-start(bf16[128,512]{1,0:T(8,128)(2,1)S(1)} %get-tuple-element.34), channel_id=1, source_target_pairs={{24,0},{26,2},{28,4},{30,6},{32,8},{34,10},{36,12},{38,14},{40,16}... | collective-permute-start | bytes 393224 | tf_op jit(solution)/shard_map/ppermute | solution.py:39
  64.1 2.6 %collective-permute-start.13 = (bf16[128,512]{1,0:T(8,128)(2,1)S(1)}, bf16[128,512]{1,0:T(8,128)(2,1)S(1)}, u32[]{:S(2)}, u32[]{:S(2)}) collective-permute-start(bf16[128,512]{1,0:T(8,128)(2,1)S(1)} %get-tuple-element.28), channel_id=1, source_target_pairs={{56,0},{58,2},{60,4},{62,6},{0,8},{2,10},{4,12},{6,14},{8,16},{10,... | collective-permute-start | bytes 393224 | tf_op jit(solution)/shard_map/ppermute | solution.py:39
  66.7 6.3 %collective-permute-done.16 = bf16[128,512]{1,0:T(8,128)(2,1)S(1)} collective-permute-done((bf16[128,512]{1,0:T(8,128)(2,1)S(1)}, bf16[128,512]{1,0:T(8,128)(2,1)S(1)}, u32[]{:S(2)}, u32[]{:S(2)}) %collective-permute-start.16) | collective-permute-done | bytes 131104 | tf_op jit(solution)/shard_map/ppermute | solution.py:39
  73.0 2.8 %collective-permute-done.13 = bf16[128,512]{1,0:T(8,128)(2,1)S(1)} collective-permute-done((bf16[128,512]{1,0:T(8,128)(2,1)S(1)}, bf16[128,512]{1,0:T(8,128)(2,1)S(1)}, u32[]{:S(2)}, u32[]{:S(2)}) %collective-permute-start.13) | collective-permute-done | bytes 131104 | tf_op jit(solution)/shard_map/ppermute | solution.py:39
  75.8 3.5 %collective-permute-done.14 = bf16[128,512]{1,0:T(8,128)(2,1)S(1)} collective-permute-done((bf16[128,512]{1,0:T(8,128)(2,1)S(1)}, bf16[128,512]{1,0:T(8,128)(2,1)S(1)}, u32[]{:S(2)}, u32[]{:S(2)}) %collective-permute-start.14) | collective-permute-done | bytes 131104 | tf_op jit(solution)/shard_map/ppermute | solution.py:39
  79.3 9.0 %collective-permute-done.15 = bf16[128,512]{1,0:T(8,128)(2,1)S(1)} collective-permute-done((bf16[128,512]{1,0:T(8,128)(2,1)S(1)}, bf16[128,512]{1,0:T(8,128)(2,1)S(1)}, u32[]{:S(2)}, u32[]{:S(2)}) %collective-permute-start.15) | collective-permute-done | bytes 131104 | tf_op jit(solution)/shard_map/ppermute | solution.py:39
  88.2 0.1 add_convert_fusion.1
  88.4 2.2 %collective-permute-start.20 = (bf16[64,512]{1,0:T(8,128)(2,1)S(1)}, bf16[64,512]{1,0:T(8,128)(2,1)S(1)}, u32[]{:S(2)}, u32[]{:S(2)}) collective-permute-start(bf16[64,512]{1,0:T(8,128)(2,1)S(1)} %broadcast_select_fusion.2), channel_id=1, source_target_pairs={{0,1},{1,0},{2,3},{3,2},{4,5},{5,4},{6,7},{7,6},{8,9},{9,8},{10,11... | collective-permute-start | bytes 196616 | tf_op jit(solution)/shard_map/ppermute | solution.py:43
  90.6 3.2 %collective-permute-start.11 = (bf16[128,1024]{1,0:T(8,128)(2,1)S(1)}, bf16[128,1024]{1,0:T(8,128)(2,1)S(1)}, u32[]{:S(2)}, u32[]{:S(2)}) collective-permute-start(bf16[128,1024]{1,0:T(8,128)(2,1)S(1)} %get-tuple-element.25), channel_id=1, source_target_pairs={{64,0},{66,2},{68,4},{70,6},{72,8},{74,10},{76,12},{78,14},{80,16}... | collective-permute-start | bytes 786440 | tf_op jit(solution)/shard_map/ppermute | solution.py:39
  93.8 0.4 collective-permute-done.20
  94.3 0.6 pad_maximum_fusion.7
  94.9 0.6 pad_maximum_fusion.6
  95.6 10.0 %collective-permute-done.10 = bf16[128,1024]{1,0:T(8,128)(2,1)S(1)} collective-permute-done((bf16[128,1024]{1,0:T(8,128)(2,1)S(1)}, bf16[128,1024]{1,0:T(8,128)(2,1)S(1)}, u32[]{:S(2)}, u32[]{:S(2)}) %collective-permute-start.10) | collective-permute-done | bytes 262176 | tf_op jit(solution)/shard_map/ppermute | solution.py:39
  105.5 0.9 add_convert_fusion
  (37 shorter events, 0.4 us)
Async XLA Ops:
  0.6 8.3 %copy-start.1 = (s32[128]{0:T(128)S(1)}, s32[128]{0:T(128)}, u32[]{:S(2)}) copy-start(s32[128]{0:T(128)} %param.14) | copy-start | bytes 1540
  2.8 23.8 %collective-permute-start = (bf16[264,1024]{1,0:T(8,128)(2,1)}, bf16[264,1024]{1,0:T(8,128)(2,1)S(1)}, u32[]{:S(2)}, u32[]{:S(2)}) collective-permute-start(bf16[264,1024]{1,0:T(8,128)(2,1)} %shard_map.103.refs_0_), channel_id=1, source_target_pairs={{64,0},{66,2},{68,4},{70,6},{72,8},{74,10},{76,12},{78,14},{80,16}... | collective-permute-start | bytes 1622024 | tf_op jit(solution)/shard_map/ppermute | solution.py:39
  5.8 15.2 %collective-permute-start.1 = (bf16[264,1024]{1,0:T(8,128)(2,1)}, bf16[264,1024]{1,0:T(8,128)(2,1)S(1)}, u32[]{:S(2)}, u32[]{:S(2)}) collective-permute-start(bf16[264,1024]{1,0:T(8,128)(2,1)} %shard_map.103.refs_0_), channel_id=1, source_target_pairs={{192,0},{194,2},{196,4},{198,6},{200,8},{202,10},{204,12},{206,14}... | collective-permute-start | bytes 1622024 | tf_op jit(solution)/shard_map/ppermute | solution.py:39
  5.8 39.5 %copy-start = (bf16[264,1024]{1,0:T(8,128)(2,1)S(1)}, bf16[264,1024]{1,0:T(8,128)(2,1)}, u32[]{:S(2)}) copy-start(bf16[264,1024]{1,0:T(8,128)(2,1)} %shard_map.103.refs_0_) | copy-start | bytes 1622020
  6.8 5.9 %collective-permute-start.4 = (bf16[64,512]{1,0:T(8,128)(2,1)S(1)}, bf16[64,512]{1,0:T(8,128)(2,1)S(1)}, u32[]{:S(2)}, u32[]{:S(2)}) collective-permute-start(bf16[64,512]{1,0:T(8,128)(2,1)S(1)} %broadcast_select_fusion.6), channel_id=1, source_target_pairs={{0,1},{1,0},{2,3},{3,2},{4,5},{5,4},{6,7},{7,6},{8,9},{9,8},{10,11... | collective-permute-start | bytes 196616 | tf_op jit(solution)/shard_map/ppermute | solution.py:43
  12.7 8.4 %collective-permute-start.5 = (bf16[136,512]{1,0:T(8,128)(2,1)S(1)}, bf16[136,512]{1,0:T(8,128)(2,1)S(1)}, u32[]{:S(2)}, u32[]{:S(2)}) collective-permute-start(bf16[136,512]{1,0:T(8,128)(2,1)S(1)} %pad_maximum_fusion.3.refs_3_.refs_2_), channel_id=1, source_target_pairs={{8,0},{10,2},{12,4},{14,6},{16,8},{18,10},{20,12},{22,14},{24,16},... | collective-permute-start | bytes 417800 | tf_op jit(solution)/shard_map/ppermute | solution.py:39
  12.9 8.9 %collective-permute-start.7 = (bf16[136,512]{1,0:T(8,128)(2,1)S(1)}, bf16[136,512]{1,0:T(8,128)(2,1)S(1)}, u32[]{:S(2)}, u32[]{:S(2)}) collective-permute-start(bf16[136,512]{1,0:T(8,128)(2,1)S(1)} %pad_maximum_fusion.3.refs_3_.refs_2_), channel_id=1, source_target_pairs={{56,0},{58,2},{60,4},{62,6},{0,8},{2,10},{4,12},{6,14},{8,16},{10,... | collective-permute-start | bytes 417800 | tf_op jit(solution)/shard_map/ppermute | solution.py:39
  21.0 28.9 %collective-permute-start.3 = (bf16[136,1024]{1,0:T(8,128)(2,1)S(1)}, bf16[136,1024]{1,0:T(8,128)(2,1)S(1)}, u32[]{:S(2)}, u32[]{:S(2)}) collective-permute-start(bf16[136,1024]{1,0:T(8,128)(2,1)S(1)} %slice.51), channel_id=1, source_target_pairs={{192,0},{194,2},{196,4},{198,6},{200,8},{202,10},{204,12},{206,14}... | collective-permute-start | bytes 835592 | tf_op jit(solution)/shard_map/ppermute | solution.py:39
  21.8 29.8 %collective-permute-start.6 = (bf16[272,512]{1,0:T(8,128)(2,1)S(1)}, bf16[272,512]{1,0:T(8,128)(2,1)S(1)}, u32[]{:S(2)}, u32[]{:S(2)}) collective-permute-start(bf16[272,512]{1,0:T(8,128)(2,1)S(1)} %get-tuple-element.40), channel_id=1, source_target_pairs={{16,0},{18,2},{20,4},{22,6},{24,8},{26,10},{28,12},{30,14},{32,16}... | collective-permute-start | bytes 835592 | tf_op jit(solution)/shard_map/ppermute | solution.py:39
  26.7 24.9 %collective-permute-start.8 = (bf16[272,512]{1,0:T(8,128)(2,1)S(1)}, bf16[272,512]{1,0:T(8,128)(2,1)S(1)}, u32[]{:S(2)}, u32[]{:S(2)}) collective-permute-start(bf16[272,512]{1,0:T(8,128)(2,1)S(1)} %get-tuple-element.39), channel_id=1, source_target_pairs={{48,0},{50,2},{52,4},{54,6},{56,8},{58,10},{60,12},{62,14},{0,16},... | collective-permute-start | bytes 835592 | tf_op jit(solution)/shard_map/ppermute | solution.py:39
  26.7 23.2 %collective-permute-start.2 = (bf16[128,1024]{1,0:T(8,128)(2,1)S(1)}, bf16[128,1024]{1,0:T(8,128)(2,1)S(1)}, u32[]{:S(2)}, u32[]{:S(2)}) collective-permute-start(bf16[128,1024]{1,0:T(8,128)(2,1)S(1)} %slice.50), channel_id=1, source_target_pairs={{64,0},{66,2},{68,4},{70,6},{72,8},{74,10},{76,12},{78,14},{80,16}... | collective-permute-start | bytes 786440 | tf_op jit(solution)/shard_map/ppermute | solution.py:39
  30.0 15.3 %collective-permute-start.9 = (bf16[136,512]{1,0:T(8,128)(2,1)S(1)}, bf16[136,512]{1,0:T(8,128)(2,1)S(1)}, u32[]{:S(2)}, u32[]{:S(2)}) collective-permute-start(bf16[136,512]{1,0:T(8,128)(2,1)S(1)} %pad_maximum_fusion.3.refs_3_.refs_2_), channel_id=1, source_target_pairs={{32,0},{34,2},{36,4},{38,6},{40,8},{42,10},{44,12},{46,14},{48,16}... | collective-permute-start | bytes 417800 | tf_op jit(solution)/shard_map/ppermute | solution.py:39
  56.1 16.9 %collective-permute-start.16 = (bf16[128,512]{1,0:T(8,128)(2,1)S(1)}, bf16[128,512]{1,0:T(8,128)(2,1)S(1)}, u32[]{:S(2)}, u32[]{:S(2)}) collective-permute-start(bf16[128,512]{1,0:T(8,128)(2,1)S(1)} %get-tuple-element.31), channel_id=1, source_target_pairs={{48,0},{50,2},{52,4},{54,6},{56,8},{58,10},{60,12},{62,14},{0,16},... | collective-permute-start | bytes 393224 | tf_op jit(solution)/shard_map/ppermute | solution.py:39
  56.1 16.8 %collective-permute-start.17 = (bf16[128,512]{1,0:T(8,128)(2,1)S(1)}, bf16[128,512]{1,0:T(8,128)(2,1)S(1)}, u32[]{:S(2)}, u32[]{:S(2)}) collective-permute-start(bf16[128,512]{1,0:T(8,128)(2,1)S(1)} %get-tuple-element.32), channel_id=1, source_target_pairs={{40,0},{42,2},{44,4},{46,6},{48,8},{50,10},{52,12},{54,14},{56,16}... | collective-permute-start | bytes 393224 | tf_op jit(solution)/shard_map/ppermute | solution.py:39
  60.6 12.4 %collective-permute-start.18 = (bf16[128,512]{1,0:T(8,128)(2,1)S(1)}, bf16[128,512]{1,0:T(8,128)(2,1)S(1)}, u32[]{:S(2)}, u32[]{:S(2)}) collective-permute-start(bf16[128,512]{1,0:T(8,128)(2,1)S(1)} %get-tuple-element.33), channel_id=1, source_target_pairs={{16,0},{18,2},{20,4},{22,6},{24,8},{26,10},{28,12},{30,14},{32,16}... | collective-permute-start | bytes 393224 | tf_op jit(solution)/shard_map/ppermute | solution.py:39
  62.4 10.6 %collective-permute-start.19 = (bf16[128,512]{1,0:T(8,128)(2,1)S(1)}, bf16[128,512]{1,0:T(8,128)(2,1)S(1)}, u32[]{:S(2)}, u32[]{:S(2)}) collective-permute-start(bf16[128,512]{1,0:T(8,128)(2,1)S(1)} %get-tuple-element.34), channel_id=1, source_target_pairs={{24,0},{26,2},{28,4},{30,6},{32,8},{34,10},{36,12},{38,14},{40,16}... | collective-permute-start | bytes 393224 | tf_op jit(solution)/shard_map/ppermute | solution.py:39
  64.1 11.7 %collective-permute-start.13 = (bf16[128,512]{1,0:T(8,128)(2,1)S(1)}, bf16[128,512]{1,0:T(8,128)(2,1)S(1)}, u32[]{:S(2)}, u32[]{:S(2)}) collective-permute-start(bf16[128,512]{1,0:T(8,128)(2,1)S(1)} %get-tuple-element.28), channel_id=1, source_target_pairs={{56,0},{58,2},{60,4},{62,6},{0,8},{2,10},{4,12},{6,14},{8,16},{10,... | collective-permute-start | bytes 393224 | tf_op jit(solution)/shard_map/ppermute | solution.py:39
  73.0 6.3 %collective-permute-start.14 = (bf16[128,512]{1,0:T(8,128)(2,1)S(1)}, bf16[128,512]{1,0:T(8,128)(2,1)S(1)}, u32[]{:S(2)}, u32[]{:S(2)}) collective-permute-start(bf16[128,512]{1,0:T(8,128)(2,1)S(1)} %get-tuple-element.29), channel_id=1, source_target_pairs={{8,0},{10,2},{12,4},{14,6},{16,8},{18,10},{20,12},{22,14},{24,16},... | collective-permute-start | bytes 393224 | tf_op jit(solution)/shard_map/ppermute | solution.py:39
  73.0 15.2 %collective-permute-start.15 = (bf16[128,512]{1,0:T(8,128)(2,1)S(1)}, bf16[128,512]{1,0:T(8,128)(2,1)S(1)}, u32[]{:S(2)}, u32[]{:S(2)}) collective-permute-start(bf16[128,512]{1,0:T(8,128)(2,1)S(1)} %get-tuple-element.30), channel_id=1, source_target_pairs={{32,0},{34,2},{36,4},{38,6},{40,8},{42,10},{44,12},{46,14},{48,16}... | collective-permute-start | bytes 393224 | tf_op jit(solution)/shard_map/ppermute | solution.py:39
  88.4 5.9 %collective-permute-start.20 = (bf16[64,512]{1,0:T(8,128)(2,1)S(1)}, bf16[64,512]{1,0:T(8,128)(2,1)S(1)}, u32[]{:S(2)}, u32[]{:S(2)}) collective-permute-start(bf16[64,512]{1,0:T(8,128)(2,1)S(1)} %broadcast_select_fusion.2), channel_id=1, source_target_pairs={{0,1},{1,0},{2,3},{3,2},{4,5},{5,4},{6,7},{7,6},{8,9},{9,8},{10,11... | collective-permute-start | bytes 196616 | tf_op jit(solution)/shard_map/ppermute | solution.py:43
  90.6 14.9 %collective-permute-start.10 = (bf16[128,1024]{1,0:T(8,128)(2,1)S(1)}, bf16[128,1024]{1,0:T(8,128)(2,1)S(1)}, u32[]{:S(2)}, u32[]{:S(2)}) collective-permute-start(bf16[128,1024]{1,0:T(8,128)(2,1)S(1)} %get-tuple-element.24), channel_id=1, source_target_pairs={{192,0},{194,2},{196,4},{198,6},{200,8},{202,10},{204,12},{206,14}... | collective-permute-start | bytes 786440 | tf_op jit(solution)/shard_map/ppermute | solution.py:39
  90.6 14.9 %collective-permute-start.11 = (bf16[128,1024]{1,0:T(8,128)(2,1)S(1)}, bf16[128,1024]{1,0:T(8,128)(2,1)S(1)}, u32[]{:S(2)}, u32[]{:S(2)}) collective-permute-start(bf16[128,1024]{1,0:T(8,128)(2,1)S(1)} %get-tuple-element.25), channel_id=1, source_target_pairs={{64,0},{66,2},{68,4},{70,6},{72,8},{74,10},{76,12},{78,14},{80,16}... | collective-permute-start | bytes 786440 | tf_op jit(solution)/shard_map/ppermute | solution.py:39
  93.8 11.7 %collective-permute-start.12 = (bf16[128,1024]{1,0:T(8,128)(2,1)S(1)}, bf16[128,1024]{1,0:T(8,128)(2,1)S(1)}, u32[]{:S(2)}, u32[]{:S(2)}) collective-permute-start(bf16[128,1024]{1,0:T(8,128)(2,1)S(1)} %get-tuple-element.26), channel_id=1, source_target_pairs={{128,0},{130,2},{132,4},{134,6},{136,8},{138,10},{140,12},{142,14}... | collective-permute-start | bytes 786440 | tf_op jit(solution)/shard_map/ppermute | solution.py:39
